TPU v7x, 512 devices: a whole 4x8x8 slice. The times are simulated.
512 devices in a mesh: tok: 32 (over z, x), vocab: 16 (over y, core).
Axes of the slice: x: 4, y: 8, z: 8, core: 2. Of those that a mesh axis runs over, the one named last changes fastest.
Arguments:
- teacher_hidden: bfloat16 [4096, 4096], P('tok', 'vocab'), may hold values from -6 to 6
- span_table: int32 [4096, 2], P('tok'), may hold values from 0 to 4096, as said below
- target_ids: int32 [4096], P('tok'), may hold values from 0 to 65535
- student_logits: bfloat16 [4096, 65536], P('tok', 'vocab')
- proj_weight: bfloat16 [1536, 4096], P('vocab')
- norm_gain: float32 [1536], replicated, may hold values from 0.1 to 1.9
- head_weight: bfloat16 [65536, 1536], P(('vocab', 'tok'))
Outputs:
- token_loss: float32 [4096], P('tok')
- proj_grad: float32 [1536, 4096], P('vocab', 'tok')
Inputs may be any that keep to these rules, and one draw needn't show every extreme that they name: `span_table`: 1 <= end - start <= 4 for every row; for the tokens of aligned block k of 128 rows, start >= k * 128 - 128 // 4 and end <= (k + 1) * 128 + 128 // 4, both reached in every block that does not touch the end of the trace.
All inputs are finite; a program needn't handle non-finite values.
Results may differ from a plain program's by a relative error of at most 0.0062.
Values may be sent and summed in bfloat16 or wider, within the bound.
A program may use at most 64 MiB of HBM per device.

v0:
```python
import jax
import jax.numpy as jnp
from jax import lax
from jax.sharding import PartitionSpec as P

EPS = 1e-06


def padded(cells, sides, width):
    for axis, dim in sides:
        count = lax.axis_size(axis)
        ends = count - 1
        head = lax.slice_in_dim(cells, 0, width, axis=dim)
        tail = lax.slice_in_dim(cells, cells.shape[dim] - width, cells.shape[dim], axis=dim)
        cells = jnp.concatenate(
            [
                lax.ppermute(tail, axis, [(i, (i + 1) % count) for i in range(ends)]),
                cells,
                lax.ppermute(head, axis, [((i + 1) % count, i) for i in range(ends)]),
            ],
            axis=dim,
        )
    return cells


def merged(value, axis, join):
    pieces = jax.tree.map(lambda part: lax.all_gather(part, axis), value)
    head = jax.tree.map(lambda part: part[0], pieces)
    tail = jax.tree.map(lambda part: part[1:], pieces)
    total, _ = lax.scan(lambda total, section: (join(total, section), None), head, tail)
    return total


def combine_stats(first, second):
    top = jnp.maximum(first[0], second[0])
    total = first[1] * jnp.exp(first[0] - top) + second[1] * jnp.exp(second[0] - top)
    return (top, total)


def local_stats(logits):
    top = jnp.max(logits, axis=1)
    return (top, jnp.sum(jnp.exp(logits - top[:, None]), axis=1))


def on_device(
    teacher_hidden, span_table, target_ids, student_logits, proj_weight, norm_gain, head_weight
):
    rows = teacher_hidden.shape[0]
    margin = rows // 4
    extended = padded(teacher_hidden, (("tok", 0),), margin)
    first_row = lax.axis_index("tok") * rows - margin
    positions = first_row + jnp.arange(rows + 2 * margin, dtype=jnp.int32)
    starts = span_table[:, 0]
    ends = span_table[:, 1]
    member = (
        (positions[None, :] >= starts[:, None]) & (positions[None, :] < ends[:, None])
    ).astype(jnp.bfloat16)
    summed = jnp.dot(member, extended, preferred_element_type=jnp.float32)
    counts = (ends - starts).astype(jnp.float32)
    pooled_part = (summed / counts[:, None]).astype(jnp.bfloat16)
    pooled = lax.all_gather(pooled_part, "vocab", axis=1, tiled=True)
    projected = lax.dot_general(
        pooled, proj_weight, (((1,), (1,)), ((), ())), preferred_element_type=jnp.float32
    )
    width_part = proj_weight.shape[0]
    width = norm_gain.shape[0]
    gain_part = lax.dynamic_slice_in_dim(
        norm_gain, lax.axis_index("vocab") * width_part, width_part
    )
    squares = lax.psum(jnp.sum(projected * projected, axis=1), "vocab")
    inverse = lax.rsqrt(squares / width + EPS)
    normed_part = (projected * inverse[:, None] * gain_part).astype(jnp.bfloat16)
    normed = lax.all_gather(normed_part, "vocab", axis=1, tiled=True)
    scaled_part = projected * inverse[:, None]
    student = student_logits.astype(jnp.float32)
    student_top, student_total = local_stats(student)
    student_top, student_total = merged((student_top, student_total), "vocab", combine_stats)
    head_full = lax.all_gather(head_weight, "tok", axis=0, tiled=True)
    head_logits = lax.dot_general(
        normed, head_full, (((1,), (1,)), ((), ())), preferred_element_type=jnp.float32
    )
    head_top, head_total = local_stats(head_logits)
    head_top, head_total = merged((head_top, head_total), "vocab", combine_stats)
    log_student = student - (student_top + jnp.log(student_total))[:, None]
    head_lse = head_top + jnp.log(head_total)
    log_head = head_logits - head_lse[:, None]
    prob_student = jnp.exp(log_student)
    prob_head = jnp.exp(log_head)
    vocab_part = student_logits.shape[1]
    vocab_ids = lax.axis_index("vocab") * vocab_part + jnp.arange(vocab_part, dtype=jnp.int32)
    hit = (vocab_ids[None, :] == target_ids[:, None]).astype(jnp.float32)
    divergence_part = jnp.sum(prob_student * (log_student - log_head), axis=1)
    picked_part = jnp.sum(hit * head_logits, axis=1)
    divergence, picked = lax.psum((divergence_part, picked_part), "vocab")
    token_loss = divergence + head_lse - picked
    logit_grad = (2.0 * prob_head - prob_student - hit).astype(jnp.bfloat16)
    columns = head_full
    normed_grad = lax.psum_scatter(
        lax.dot_general(
            columns, logit_grad, (((0,), (1,)), ((), ())), preferred_element_type=jnp.float32
        ),
        "vocab",
        scatter_dimension=0,
        tiled=True,
    ).T
    gain_grad = normed_grad * gain_part
    inner = lax.psum(jnp.sum(gain_grad * scaled_part, axis=1), "vocab")
    out_grad = (inverse[:, None] * (gain_grad - scaled_part * inner[:, None] / width)).astype(
        jnp.bfloat16
    )
    columns = pooled
    grad_rows = lax.psum_scatter(
        lax.dot_general(
            columns, out_grad, (((0,), (0,)), ((), ())), preferred_element_type=jnp.float32
        ),
        "tok",
        scatter_dimension=0,
        tiled=True,
    )
    return (token_loss, grad_rows.T)


def solution(mesh):
    return jax.shard_map(
        on_device,
        mesh=mesh,
        in_specs=(
            P("tok", "vocab"),
            P("tok", None),
            P("tok"),
            P("tok", "vocab"),
            P("vocab", None),
            P(),
            P(("vocab", "tok"), None),
        ),
        out_specs=(P("tok"), P("vocab", "tok")),
        check_vma=False,
    )
```

profile of v0, /device:TPU:1, one launch (start us, length us, event | category | flops | bytes accessed | tf_op | source)
XLA Modules:
  0.0 557.3 jit_solution(11921284806211572373)
XLA Ops:
  7.2 0.0 copy-start
  7.2 0.0 copy-start.1
  7.2 0.0 all-gather.11.cloned.1.call-start
  7.2 0.9 fusion.52
  8.1 3.9 collective-permute-start
  12.0 1.3 collective-permute-start.1
  13.3 0.8 slice_bitcast_fusion.5
  14.1 0.0 collective-permute-done
  14.1 2.4 collective-permute-done.1
  16.5 1.7 fusion.20
  18.2 0.0 all-gather.11.cloned.1.call-update
  18.2 0.0 all-gather.13.cloned.1.call-start
  18.3 0.7 all-gather.13.cloned.1.call-update
  19.0 0.0 reduce-scatter.3.cloned.1.call-start
  19.0 0.0 copy-done.1
  19.0 0.2 reduce_max.27
  19.3 0.5 fusion.18
  19.8 19.5 %all-gather.5 = f32[16,1,128]{2,1,0:T(1,128)S(1)} all-gather(f32[1,1,128]{2,1,0:T(1,128)S(1)} %bitcast.85), channel_id=3, replica_groups=mesh['tok'=32,'vocab'=16] {'vocab'}, dimensions={0}, use_global_device_ids=true | all-gather | bytes 8704 | tf_op jit(solution)/shard_map/all_gather | solution.py:27
  39.3 15.9 %all-gather.4 = f32[16,1,128]{2,1,0:T(1,128)S(1)} all-gather(f32[1,1,128]{2,1,0:T(1,128)S(1)} %get-tuple-element.97), channel_id=2, replica_groups=mesh['tok'=32,'vocab'=16] {'vocab'}, dimensions={0}, use_global_device_ids=true | all-gather | bytes 8704 | tf_op jit(solution)/shard_map/all_gather | solution.py:27
  55.2 0.8 dynamic_slice.16
  56.0 0.6 while.24
  56.6 10.1 %all-gather.11.cloned.1.call-done = bf16[128,4096]{1,0:T(8,128)(2,1)} async-done(((bf16[128,256]{1,0:T(8,128)(2,1)}), bf16[128,4096]{1,0:T(8,128)(2,1)}) %all-gather.11.cloned.1.call-update) | async-done | bytes 1048592 | tf_op jit(solution)/shard_map/all_gather | solution.py:61
  66.7 0.0 copy-done
  66.7 1.7 multiply_reduce_fusion
  68.4 23.2 %psum.28 = f32[128]{0:T(128)S(1)} all-reduce(f32[128]{0:T(128)S(1)} %get-tuple-element.98), channel_id=1, replica_groups=mesh['tok'=32,'vocab'=16] {'vocab'}, use_global_device_ids=true, to_apply=%region_5.6 | all-reduce | flops 128 | bytes 1024 | tf_op jit(solution)/shard_map/psum | solution.py:70
  91.6 0.1 multiply_convert_fusion
  91.7 18.7 %all_gather.35 = bf16[128,1536]{0,1:T(8,128)(2,1)S(1)} all-gather(bf16[128,96]{0,1:T(8,128)(2,1)S(1)} %multiply_convert_fusion), channel_id=1, replica_groups=mesh['tok'=32,'vocab'=16] {'vocab'}, dimensions={1}, use_global_device_ids=true | all-gather | bytes 417792 | tf_op jit(solution)/shard_map/all_gather | solution.py:73
  110.4 82.9 %all-gather.13.cloned.1.call-done = bf16[4096,1536]{1,0:T(8,128)(2,1)} async-done(((bf16[128,1536]{1,0:T(8,128)(2,1)}), bf16[4096,1536]{1,0:T(8,128)(2,1)}) %all-gather.13.cloned.1.call-update) | async-done | bytes 12582928 | tf_op jit(solution)/shard_map/all_gather | solution.py:78
  193.2 8.8 %fusion.54 = (f32[128]{0:T(128)S(1)}, f32[128,4096]{1,0:T(8,128)S(1)}) fusion(bf16[128,1536]{0,1:T(8,128)(2,1)S(1)} %all_gather.35, bf16[4096,1536]{1,0:T(8,128)(2,1)} %all-gather.13.cloned.1.call-done), kind=kOutput, calls=%fused_computation.83 | convolution fusion | flops 1611136896 | bytes 15073792 | tf_op jit(solution)/shard_map/dot_general | solution.py:79
  202.1 0.0 copy-start.2
  202.1 0.4 exponential_reduce_fusion
  202.5 18.2 %all-gather.7 = f32[16,1,128]{2,1,0:T(1,128)S(1)} all-gather(f32[1,1,128]{2,1,0:T(1,128)S(1)} %bitcast.86), channel_id=5, replica_groups=mesh['tok'=32,'vocab'=16] {'vocab'}, dimensions={0}, use_global_device_ids=true | all-gather | bytes 8704 | tf_op jit(solution)/shard_map/all_gather | solution.py:27
  220.7 15.2 %all-gather.6 = f32[16,1,128]{2,1,0:T(1,128)S(1)} all-gather(f32[1,1,128]{2,1,0:T(1,128)S(1)} %bitcast.84), channel_id=4, replica_groups=mesh['tok'=32,'vocab'=16] {'vocab'}, dimensions={0}, use_global_device_ids=true | all-gather | bytes 8704 | tf_op jit(solution)/shard_map/all_gather | solution.py:27
  235.9 0.6 while.25
  236.5 0.0 copy-done.2
  236.5 11.1 %convolution_bitcast_fusion = f32[1536,128]{1,0:T(8,128)} fusion(bf16[4096,1536]{1,0:T(8,128)(2,1)} %all-gather.13.cloned.1.call-done, bf16[128,4096]{1,0:T(8,128)(2,1)} %param.14, f32[128,4096]{1,0:T(8,128)S(1)} %get-tuple-element.101, s32[4096]{0:T(1024)S(1)} %iota_add_fusion, f32[128]{0:T(128)S(1)} %log_add_fusion, f32[128]{0:T(128)S(1)} %log_add_fusion.1, ...), kind=kOutput, calls=%fused_computation.20 | convolution fusion | flops 1615331328 | bytes 16532992 | tf_op jit(solution)/shard_map/dot_general | solution.py:99
  247.6 0.0 reduce-scatter.3.cloned.1.call-update
  247.7 0.0 reduce-scatter.5.cloned.1.call-start
  247.7 2.1 fusion.14
  249.8 50.6 %reduce-scatter.3.cloned.1.call-done = f32[96,128]{1,0:T(8,128)} async-done(((f32[1536,128]{1,0:T(8,128)}), f32[96,128]{1,0:T(8,128)}) %reduce-scatter.3.cloned.1.call-update) | async-done | bytes 49168 | tf_op jit(solution)/shard_map/reduce_scatter | solution.py:98
  300.4 0.9 fusion.38
  301.3 25.2 %all-reduce = (f32[128]{0:T(128)S(1)}, f32[128]{0:T(128)S(1)}, f32[128]{0:T(128)S(1)}) all-reduce(f32[128]{0:T(128)S(1)} %get-tuple-element.63, f32[128]{0:T(128)S(1)} %get-tuple-element.62, f32[128]{0:T(128)S(1)} %fusion.38), channel_id=1, replica_groups=mesh['tok'=32,'vocab'=16] {'vocab'}, use_global_device_ids=true, to_apply=%region_13.14 | all-reduce | flops 384 | bytes 3072 | tf_op jit(solution)/shard_map/psum | solution.py:94
  326.5 2.8 fusion.41
  329.3 0.0 reduce-scatter.5.cloned.1.call-update
  329.3 0.5 add_subtract_fusion
  329.8 220.9 %reduce-scatter.5.cloned.1.call-done = f32[128,96]{0,1:T(8,128)} async-done(((f32[4096,96]{0,1:T(8,128)}), f32[128,96]{0,1:T(8,128)}) %reduce-scatter.5.cloned.1.call-update) | async-done | bytes 49168 | tf_op jit(solution)/shard_map/reduce_scatter | solution.py:112
  (48 shorter events, 0.9 us)
Async XLA Ops:
  7.2 59.5 %copy-start = (bf16[96,4096]{1,0:T(8,128)(2,1)S(1)}, bf16[96,4096]{1,0:T(8,128)(2,1)}, u32[]{:S(2)}) copy-start(bf16[96,4096]{1,0:T(8,128)(2,1)} %param.15) | copy-start | bytes 2359300
  7.2 11.8 %copy-start.1 = (bf16[128,4096]{1,0:T(8,128)(2,1)S(1)}, bf16[128,4096]{1,0:T(8,128)(2,1)}, u32[]{:S(2)}) copy-start(bf16[128,4096]{1,0:T(8,128)(2,1)} %param.14) | copy-start | bytes 3145732
  7.2 59.5 %all-gather.11.cloned.1.call-start = ((), (), s32[]{:S(2)}) async-start(), calls=%async_computation.2 | async-start | bytes 1114112 | tf_op jit(solution)/shard_map/all_gather | solution.py:61
  8.1 6.0 %collective-permute-start = (bf16[32,256]{1,0:T(8,128)(2,1)S(1)}, bf16[32,256]{1,0:T(8,128)(2,1)S(1)}, u32[]{:S(2)}, u32[]{:S(2)}) collective-permute-start(bf16[32,256]{1,0:T(8,128)(2,1)S(1)} %get-tuple-element.91), channel_id=1, source_target_pairs={{0,16},{16,32},{32,48},{48,64},{64,80},{80,96},{96,112},{112,128},... | collective-permute-start | bytes 49160 | tf_op jit(solution)/shard_map/ppermute | solution.py:17
  12.0 4.5 collective-permute-start.1
  18.2 175.0 %all-gather.13.cloned.1.call-start = ((), (), s32[]{:S(2)}) async-start(), calls=%async_computation.3 | async-start | bytes 12976128 | tf_op jit(solution)/shard_map/all_gather | solution.py:78
  19.0 281.4 %reduce-scatter.3.cloned.1.call-start = ((), (), s32[]{:S(2)}) async-start(), calls=%async_computation.4 | async-start | bytes 835584 | tf_op jit(solution)/shard_map/reduce_scatter | solution.py:98
  202.1 34.5 %copy-start.2 = (s32[128]{0:T(128)S(1)}, s32[128]{0:T(128)}, u32[]{:S(2)}) copy-start(s32[128]{0:T(128)} %param.13) | copy-start | bytes 1540
  247.7 303.1 %reduce-scatter.5.cloned.1.call-start = ((), (), s32[]{:S(2)}) async-start(), calls=%async_computation.5 | async-start | bytes 1622016 | tf_op jit(solution)/shard_map/reduce_scatter | solution.py:112
Sparse Core Ops, SparseCore 0:
  18.3 48.3 all-gather.10
  69.8 123.3 all-gather.12
  247.8 52.5 reduce-scatter.2
  329.4 221.2 reduce-scatter.4
where the time goes:
time: 562 us; the launch traced here: 557 us
  waiting for transfers between devices  368 us (65%)
  blocking collectives  136 us (24%)
  matrix products  26.1 us (5%)
  between operations  13.9 us (2%)
  other arithmetic  6.39 us (1%)
    reduce_scatter x1, waiting for transfers between devices, on_device(): lax.psum_scatter(lax.dot_general(columns, out_grad, (((0,), (0,)), ((), (...  221 us
    all_gather x1, waiting for transfers between devices, on_device(): head_full = lax.all_gather(head_weight, 'tok', axis=0, tiled=True)  82.9 us
    all_gather x4, blocking collectives, merged(): pieces = jax.tree.map(lambda part: lax.all_gather(part, axis), value)  68.8 us
    reduce_scatter x1, waiting for transfers between devices, on_device(): lax.psum_scatter(lax.dot_general(columns, logit_grad, (((0,), (1,)), ((),...  50.6 us
    psum x1, blocking collectives, on_device(): divergence, picked = lax.psum((divergence_part, picked_part), 'vocab')  25.2 us
    psum x1, blocking collectives, on_device(): squares = lax.psum(jnp.sum(projected * projected, axis=1), 'vocab')  23.2 us
    all_gather x1, blocking collectives, on_device(): normed = lax.all_gather(normed_part, 'vocab', axis=1, tiled=True)  18.7 us
  transfers between devices with their start and end apart: 6, of which 5 were waited for; matrix products, arithmetic and copies ran while one was open for 1% of the time, Pallas kernels for 0%

commit v1 on v0

v1 whole, which is shorter than its diff:
```python
import functools

import jax
import jax.numpy as jnp
from jax import lax
from jax.experimental import pallas as pl
from jax.experimental.pallas import tpu as pltpu
from jax.sharding import PartitionSpec as P

EPS = 1e-06
MESH = pl.DeviceIdType.MESH


def greet(peers):
    barrier = pltpu.get_barrier_semaphore()
    for peer in peers:
        pl.semaphore_signal(barrier, inc=1, device_id={"vocab": peer}, device_id_type=MESH)
    pl.semaphore_wait(barrier, len(peers))


def gather_kernel(chips, block, out, send, recv, pass_send, pass_recv, keep):
    me = lax.axis_index("vocab")
    core = lax.rem(me, 2)
    chip = lax.div(me, 2)
    partner = chip * 2 + (1 - core)
    ahead = [lax.rem(chip + step, chips) * 2 + core for step in range(1, chips)]
    behind = [lax.rem(chip + chips - step, chips) * 2 + core for step in range(1, chips)]
    greet(ahead + [partner])
    steps = sorted(range(1, chips), key=lambda step: -min(step, chips - step))
    copies = {}
    for step in steps:
        copies[step] = pltpu.make_async_remote_copy(
            src_ref=block, dst_ref=out.at[me], send_sem=send.at[step], recv_sem=recv.at[step],
            device_id={"vocab": ahead[step - 1]}, device_id_type=MESH,
        )
        copies[step].start()
    own = pltpu.make_async_copy(block, out.at[me], keep)
    own.start()
    passes = [
        pltpu.make_async_remote_copy(
            src_ref=block, dst_ref=out.at[me], send_sem=pass_send.at[0], recv_sem=pass_recv.at[0],
            device_id={"vocab": partner}, device_id_type=MESH,
        )
    ]
    passes[0].start()
    for step in reversed(steps):
        copies[step].wait_recv()
        source = behind[step - 1]
        onward = pltpu.make_async_remote_copy(
            src_ref=out.at[source], dst_ref=out.at[source],
            send_sem=pass_send.at[step], recv_sem=pass_recv.at[step],
            device_id={"vocab": partner}, device_id_type=MESH,
        )
        onward.start()
        passes.append(onward)
    for onward in passes:
        onward.wait()
    for step in steps:
        copies[step].wait_send()
    own.wait()


def vocab_gather(block, collective_id):
    count = lax.axis_size("vocab")
    chips = count // 2
    return pl.pallas_call(
        functools.partial(gather_kernel, chips),
        out_shape=jax.ShapeDtypeStruct((count,) + block.shape, block.dtype),
        in_specs=[pl.BlockSpec(memory_space=pltpu.VMEM)],
        out_specs=pl.BlockSpec(memory_space=pltpu.VMEM),
        scratch_shapes=[pltpu.SemaphoreType.DMA((chips,))] * 4 + [pltpu.SemaphoreType.DMA],
        compiler_params=pltpu.CompilerParams(collective_id=collective_id, has_side_effects=True),
        cost_estimate=pl.CostEstimate(flops=0, bytes_accessed=30_000_000, transcendentals=0),
    )(block)


def exchange_kernel(count, blocks, out, send, recv, keep):
    me = lax.axis_index("vocab")
    ahead = [lax.rem(me + step, count) for step in range(1, count)]
    greet(ahead)
    own = pltpu.make_async_copy(blocks.at[me], out.at[me], keep)
    own.start()
    copies = []
    for step in sorted(range(1, count), key=lambda step: -min(step, count - step)):
        copy = pltpu.make_async_remote_copy(
            src_ref=blocks.at[ahead[step - 1]], dst_ref=out.at[me],
            send_sem=send.at[step], recv_sem=recv.at[step],
            device_id={"vocab": ahead[step - 1]}, device_id_type=MESH,
        )
        copy.start()
        copies.append(copy)
    for copy in copies:
        copy.wait()
    own.wait()


def vocab_exchange(blocks, collective_id):
    count = lax.axis_size("vocab")
    return pl.pallas_call(
        functools.partial(exchange_kernel, count),
        out_shape=jax.ShapeDtypeStruct(blocks.shape, blocks.dtype),
        in_specs=[pl.BlockSpec(memory_space=pltpu.VMEM)],
        out_specs=pl.BlockSpec(memory_space=pltpu.VMEM),
        scratch_shapes=[pltpu.SemaphoreType.DMA((count,))] * 2 + [pltpu.SemaphoreType.DMA],
        compiler_params=pltpu.CompilerParams(collective_id=collective_id, has_side_effects=True),
        cost_estimate=pl.CostEstimate(flops=0, bytes_accessed=30_000_000, transcendentals=0),
    )(blocks)


def padded(cells, axis, width):
    count = lax.axis_size(axis)
    ends = count - 1
    head = cells[:width]
    tail = cells[cells.shape[0] - width :]
    return jnp.concatenate(
        [
            lax.ppermute(tail, axis, [(i, (i + 1) % count) for i in range(ends)]),
            cells,
            lax.ppermute(head, axis, [((i + 1) % count, i) for i in range(ends)]),
        ],
        axis=0,
    )


def on_device(
    teacher_hidden, span_table, target_ids, student_logits, proj_weight, norm_gain, head_weight
):
    n_tok = lax.axis_size("tok")
    n_vocab = lax.axis_size("vocab")
    head_full = lax.all_gather(head_weight, "tok", axis=0, tiled=True)
    rows = teacher_hidden.shape[0]
    margin = rows // 4
    extended = padded(teacher_hidden, "tok", margin)
    first_row = lax.axis_index("tok") * rows - margin
    positions = first_row + jnp.arange(rows + 2 * margin, dtype=jnp.int32)
    starts = span_table[:, 0]
    ends = span_table[:, 1]
    member = (
        (positions[None, :] >= starts[:, None]) & (positions[None, :] < ends[:, None])
    ).astype(jnp.bfloat16)
    summed = jnp.dot(member, extended, preferred_element_type=jnp.float32)
    counts = (ends - starts).astype(jnp.float32)
    pooled_part = (summed / counts[:, None]).astype(jnp.bfloat16)
    part = pooled_part.shape[1]
    pooled = vocab_gather(pooled_part, 0)
    pooled = jnp.swapaxes(pooled, 0, 1).reshape(rows, n_vocab * part)
    projected_part = lax.dot_general(
        proj_weight, pooled, (((1,), (1,)), ((), ())), preferred_element_type=jnp.float32
    )
    width_part = proj_weight.shape[0]
    width = norm_gain.shape[0]
    projected = vocab_gather(projected_part, 1).reshape(width, rows)
    inverse = lax.rsqrt(jnp.sum(projected * projected, axis=0) / width + EPS)
    normed = (projected * inverse[None, :] * norm_gain[:, None]).astype(jnp.bfloat16)
    column_part = n_vocab * part // n_tok
    pooled_columns = lax.all_to_all(
        pooled.reshape(rows, n_tok, column_part), "tok", 1, 0, tiled=True
    ).reshape(n_tok * rows, column_part)

    student = student_logits.astype(jnp.float32)
    head_logits = lax.dot_general(
        normed, head_full, (((0,), (1,)), ((), ())), preferred_element_type=jnp.float32
    )
    vocab_part = student_logits.shape[1]
    vocab_ids = lax.axis_index("vocab") * vocab_part + jnp.arange(vocab_part, dtype=jnp.int32)
    hit = (vocab_ids[None, :] == target_ids[:, None]).astype(jnp.float32)
    student_top = jnp.max(student, axis=1)
    student_exp = jnp.exp(student - student_top[:, None])
    head_top = jnp.max(head_logits, axis=1)
    head_exp = jnp.exp(head_logits - head_top[:, None])
    stats = jnp.stack(
        [
            student_top,
            jnp.sum(student_exp, axis=1),
            jnp.sum(student_exp * (student - head_logits), axis=1),
            jnp.sum(student_exp * head_logits, axis=1),
            head_top,
            jnp.sum(head_exp, axis=1),
            jnp.sum(head_exp * head_logits, axis=1),
            jnp.sum(hit * head_logits, axis=1),
        ]
    )
    stats = vocab_gather(stats, 2)
    tops = jnp.max(stats, axis=0)
    student_scale = jnp.exp(stats[:, 0] - tops[0])
    head_scale = jnp.exp(stats[:, 4] - tops[4])
    student_total = jnp.sum(stats[:, 1] * student_scale, axis=0)
    student_gap = jnp.sum(stats[:, 2] * student_scale, axis=0) / student_total
    student_head = jnp.sum(stats[:, 3] * student_scale, axis=0) / student_total
    head_total = jnp.sum(stats[:, 5] * head_scale, axis=0)
    head_head = jnp.sum(stats[:, 6] * head_scale, axis=0) / head_total
    picked = jnp.sum(stats[:, 7], axis=0)
    student_lse = tops[0] + jnp.log(student_total)
    head_lse = tops[4] + jnp.log(head_total)
    token_loss = student_gap - student_lse + head_lse + head_lse - picked
    inner = 2.0 * head_head - student_head - picked

    prob_student = jnp.exp(student - student_lse[:, None])
    prob_head = jnp.exp(head_logits - head_lse[:, None])
    logit_grad = (2.0 * prob_head - prob_student - hit).astype(jnp.bfloat16)
    grad_parts = lax.dot_general(
        head_full, logit_grad, (((0,), (1,)), ((), ())), preferred_element_type=jnp.float32
    ).astype(jnp.bfloat16)
    grad_parts = vocab_exchange(grad_parts.reshape(n_vocab, width_part, rows), 3)
    normed_grad = jnp.sum(grad_parts.astype(jnp.float32), axis=0)
    gain_part = lax.dynamic_slice_in_dim(
        norm_gain, lax.axis_index("vocab") * width_part, width_part
    )
    gain_grad = normed_grad * gain_part[:, None]
    scaled_part = projected_part * inverse[None, :]
    out_grad = (inverse[None, :] * (gain_grad - scaled_part * inner[None, :] / width)).astype(
        jnp.bfloat16
    )
    out_grads = lax.all_gather(out_grad, "tok", axis=0)
    out_grads = jnp.swapaxes(out_grads, 0, 1).reshape(width_part, n_tok * rows)
    proj_grad = jnp.dot(out_grads, pooled_columns, preferred_element_type=jnp.float32)
    return (token_loss, proj_grad)


def solution(mesh):
    return jax.shard_map(
        on_device,
        mesh=mesh,
        in_specs=(
            P("tok", "vocab"),
            P("tok", None),
            P("tok"),
            P("tok", "vocab"),
            P("vocab", None),
            P(),
            P(("vocab", "tok"), None),
        ),
        out_specs=(P("tok"), P("vocab", "tok")),
        check_vma=False,
    )
```

time: 562 us -> 254 us (0.45)
  the two profiles are of different devices: /device:TPU:1 before, /device:TPU:8 now
where the time goes in v1:
time: 254 us; the launch traced here: 253 us
  waiting for transfers between devices  68 us (27%)
  Pallas kernels  65.9 us (26%)
  blocking collectives  48.2 us (19%)
  matrix products  20.9 us (8%)
  starting transfers between devices  19.8 us (8%)
  between operations  14.2 us (6%)
  other arithmetic  9.31 us (4%)
  local copies, waits for them, and re-layouts  6.47 us (3%)
    all_gather x1, waiting for transfers between devices, on_device(): head_full = lax.all_gather(head_weight, 'tok', axis=0, tiled=True)  55.3 us
    pallas_call x3, Pallas kernels, vocab_gather(): pl.pallas_call(functools.partial(gather_kernel, chips), out_shape=jax.Sha...  48.7 us
    all_gather x1, blocking collectives, on_device(): out_grads = lax.all_gather(out_grad, 'tok', axis=0)  48.2 us
    pallas_call x1, Pallas kernels, vocab_exchange(): pl.pallas_call(functools.partial(exchange_kernel, count), out_shape=jax.S...  17.1 us
    all_to_all x1, starting transfers between devices, on_device(): lax.all_to_all(pooled.reshape(rows, n_tok, column_part), 'tok', 1, 0, til...  15.1 us
    dot_general x1, matrix products, on_device(): lax.dot_general(normed, head_full, (((0,), (1,)), ((), ())), preferred_el...  8.9 us
    all_to_all x1, waiting for transfers between devices, on_device(): lax.all_to_all(pooled.reshape(rows, n_tok, column_part), 'tok', 1, 0, til...  8.49 us
    dot_general x1, matrix products, on_device(): lax.dot_general(head_full, logit_grad, (((0,), (1,)), ((), ())), preferre...  7.05 us
  transfers between devices with their start and end apart: 4, of which 3 were waited for; matrix products, arithmetic and copies ran while one was open for 5% of the time, Pallas kernels for 15%

profile of v1, /device:TPU:8, one launch (start us, length us, event | category | flops | bytes accessed | tf_op | source)
XLA Modules:
  0.0 252.9 jit_solution(3634911712474533478)
XLA Ops:
  7.2 0.0 copy-start
  7.2 0.0 all-gather.3.cloned.1.call-start
  7.2 0.7 all-gather.3.cloned.1.call-update
  7.9 0.7 fusion.40
  8.7 3.4 %collective-permute-start = (bf16[32,256]{1,0:T(8,128)(2,1)S(1)}, bf16[32,256]{1,0:T(8,128)(2,1)S(1)}, u32[]{:S(2)}, u32[]{:S(2)}) collective-permute-start(bf16[32,256]{1,0:T(8,128)(2,1)S(1)} %get-tuple-element.25), channel_id=1, source_target_pairs={{0,16},{16,32},{32,48},{48,64},{64,80},{80,96},{96,112},{112,128},... | collective-permute-start | bytes 49160 | tf_op jit(solution)/shard_map/ppermute | solution.py:117
  12.0 1.3 collective-permute-start.1
  13.4 0.8 slice_bitcast_fusion.3
  14.1 0.0 collective-permute-done
  14.1 3.6 %collective-permute-done.1 = bf16[32,256]{1,0:T(8,128)(2,1)S(1)} collective-permute-done((bf16[32,256]{1,0:T(8,128)(2,1)S(1)}, bf16[32,256]{1,0:T(8,128)(2,1)S(1)}, u32[]{:S(2)}, u32[]{:S(2)}) %collective-permute-start.1) | collective-permute-done | bytes 16416 | tf_op jit(solution)/shard_map/ppermute | solution.py:119
  17.7 1.7 fusion.13.block
  19.4 20.7 %shard_map.86 = bf16[16,128,256]{2,1,0:T(8,128)(2,1)} custom-call(bf16[128,256]{1,0:T(8,128)(2,1)} %fusion.13.block), custom_call_target="tpu_custom_call" | custom-call | bytes 30000000 | tf_op jit(solution)/shard_map/pallas_call | solution.py:66
  40.1 0.0 copy-start.5
  40.1 0.0 copy-start.2
  40.1 2.4 copy.15
  42.5 15.1 %all-to-all-start = ((bf16[128,32,128]{0,2,1:T(8,128)(2,1)}), bf16[128,32,128]{0,2,1:T(8,128)(2,1)S(1)}, u32[]{:S(2)}, u32[]{:S(2)}) async-start(bf16[128,32,128]{0,2,1:T(8,128)(2,1)} %bitcast.28), calls=%async_computation | async-start | bytes 2097152 | tf_op jit(solution)/shard_map/all_to_all | solution.py:156
  57.7 0.0 copy-done.5
  57.7 0.1 dynamic_slice.3
  57.8 0.0 copy-done.2
  57.8 0.2 reduce_max.36
  58.0 0.0 copy-done
  58.0 2.2 convolution_bitcast_fusion.block
  60.2 17.3 %shard_map.87 = f32[16,96,128]{2,1,0:T(8,128)} custom-call(f32[96,128]{1,0:T(8,128)} %convolution_bitcast_fusion.block), custom_call_target="tpu_custom_call" | custom-call | bytes 30000000 | tf_op jit(solution)/shard_map/pallas_call | solution.py:66
  77.6 1.4 multiply_reduce_fusion.1
  78.9 1.4 fusion.24
  80.3 8.5 %all-to-all-done = bf16[128,32,128]{0,2,1:T(8,128)(2,1)S(1)} async-done(((bf16[128,32,128]{0,2,1:T(8,128)(2,1)}), bf16[128,32,128]{0,2,1:T(8,128)(2,1)S(1)}, u32[]{:S(2)}, u32[]{:S(2)}) %all-to-all-start) | async-done | bytes 1048608 | tf_op jit(solution)/shard_map/all_to_all | solution.py:156
  88.8 1.4 copy.24
  90.2 0.0 copy-start.6
  90.2 55.3 %all-gather.3.cloned.1.call-done = bf16[4096,1536]{1,0:T(8,128)(2,1)} async-done(((bf16[128,1536]{1,0:T(8,128)(2,1)}), bf16[4096,1536]{1,0:T(8,128)(2,1)}) %all-gather.3.cloned.1.call-update) | async-done | bytes 12582928 | tf_op jit(solution)/shard_map/all_gather | solution.py:130
  145.5 8.9 %fusion.42 = (f32[128]{0:T(128)S(1)}, f32[128,4096]{1,0:T(8,128)S(1)}) fusion(bf16[1536,128]{1,0:T(8,128)(2,1)S(1)} %fusion.24, bf16[4096,1536]{1,0:T(8,128)(2,1)} %all-gather.3.cloned.1.call-done), kind=kOutput, calls=%fused_computation.76 | convolution fusion | flops 1611136896 | bytes 15073792 | tf_op jit(solution)/shard_map/dot_general | solution.py:161
  154.4 0.0 copy-done.6
  154.4 0.0 copy-done.3
  154.4 1.7 multiply_reduce_fusion
  156.1 0.6 stack.32.block
  156.7 10.7 %shard_map.88 = f32[16,8,128]{2,1,0:T(8,128)} custom-call(f32[8,128]{1,0:T(8,128)} %stack.32.block), custom_call_target="tpu_custom_call" | custom-call | bytes 30000000 | tf_op jit(solution)/shard_map/pallas_call | solution.py:66
  167.4 1.3 fusion.39
  168.7 0.9 reduce_max.41
  169.6 0.5 fusion.36
  170.1 7.0 %fusion = bf16[1536,128]{0,1:T(8,128)(2,1)S(1)} fusion(bf16[4096,1536]{1,0:T(8,128)(2,1)} %all-gather.3.cloned.1.call-done, bf16[128,4096]{1,0:T(8,128)(2,1)} %param.10, f32[128,4096]{1,0:T(8,128)S(1)} %get-tuple-element.37, f32[128]{0:T(128)S(1)} %get-tuple-element.27, f32[128]{0:T(128)S(1)} %get-tuple-element.16, s32[4096]{0:T(1024)S(1)} %iota_add_fusion, ...), kind=kOutput, calls=%fused_computation.6 | convolution fusion | flops 1615527936 | bytes 16139776 | tf_op jit(solution)/shard_map/dot_general | solution.py:201
  177.2 0.0 copy-start.1
  177.2 0.9 copy.21
  178.1 17.1 %shard_map.89 = bf16[16,96,128]{2,1,0:T(8,128)(2,1)} custom-call(bf16[16,96,128]{2,1,0:T(8,128)(2,1)} %bitcast.78), custom_call_target="tpu_custom_call" | custom-call | bytes 30000000 | tf_op jit(solution)/shard_map/pallas_call | solution.py:99
  195.3 1.1 convert_reduce_fusion
  196.3 0.0 copy-done.4
  196.3 0.1 multiply_convert_fusion
  196.4 48.2 %all-gather = bf16[3072,128]{1,0:T(8,128)(2,1)S(1)} all-gather(bf16[96,128]{1,0:T(8,128)(2,1)S(1)} %multiply_convert_fusion), channel_id=2, replica_groups=mesh['tok'=32,'vocab'=16] {'tok'}, dimensions={0}, use_global_device_ids=true | all-gather | bytes 811008 | tf_op jit(solution)/shard_map/all_gather | solution.py:214
  244.6 0.3 copy.22
  244.9 0.0 copy-done.1
  244.9 1.1 fusion.20
  (8 shorter events, 0.1 us)
Async XLA Ops:
  7.2 50.8 %copy-start = (bf16[96,4096]{1,0:T(8,128)(2,1)S(1)}, bf16[96,4096]{1,0:T(8,128)(2,1)}, u32[]{:S(2)}) copy-start(bf16[96,4096]{1,0:T(8,128)(2,1)} %param.11) | copy-start | bytes 2359300
  7.2 138.3 %all-gather.3.cloned.1.call-start = ((), (), s32[]{:S(2)}) async-start(), calls=%async_computation.1 | async-start | bytes 12976128 | tf_op jit(solution)/shard_map/all_gather | solution.py:130
  8.7 5.5 %collective-permute-start = (bf16[32,256]{1,0:T(8,128)(2,1)S(1)}, bf16[32,256]{1,0:T(8,128)(2,1)S(1)}, u32[]{:S(2)}, u32[]{:S(2)}) collective-permute-start(bf16[32,256]{1,0:T(8,128)(2,1)S(1)} %get-tuple-element.25), channel_id=1, source_target_pairs={{0,16},{16,32},{32,48},{48,64},{64,80},{80,96},{96,112},{112,128},... | collective-permute-start | bytes 49160 | tf_op jit(solution)/shard_map/ppermute | solution.py:117
  12.0 5.6 %collective-permute-start.1 = (bf16[32,256]{1,0:T(8,128)(2,1)S(1)}, bf16[32,256]{1,0:T(8,128)(2,1)S(1)}, u32[]{:S(2)}, u32[]{:S(2)}) collective-permute-start(bf16[32,256]{1,0:T(8,128)(2,1)S(1)} %get-tuple-element.26), channel_id=1, source_target_pairs={{16,0},{32,16},{48,32},{64,48},{80,64},{96,80},{112,96},{128,112},... | collective-permute-start | bytes 49160 | tf_op jit(solution)/shard_map/ppermute | solution.py:119
  40.1 17.6 %copy-start.5 = (f32[1536]{0:T(1024)S(1)}, f32[1536]{0:T(1024)}, u32[]{:S(2)}) copy-start(f32[1536]{0:T(1024)} %param.12) | copy-start | bytes 18436
  40.1 17.7 %copy-start.2 = (bf16[128,4096]{1,0:T(8,128)(2,1)S(1)}, bf16[128,4096]{1,0:T(8,128)(2,1)}, u32[]{:S(2)}) copy-start(bf16[128,4096]{1,0:T(8,128)(2,1)} %param.10) | copy-start | bytes 3145732
  42.5 46.3 %all-to-all-start = ((bf16[128,32,128]{0,2,1:T(8,128)(2,1)}), bf16[128,32,128]{0,2,1:T(8,128)(2,1)S(1)}, u32[]{:S(2)}, u32[]{:S(2)}) async-start(bf16[128,32,128]{0,2,1:T(8,128)(2,1)} %bitcast.28), calls=%async_computation | async-start | bytes 2097152 | tf_op jit(solution)/shard_map/all_to_all | solution.py:156
  90.2 64.2 %copy-start.6 = (s32[128]{0:T(128)S(1)}, s32[128]{0:T(128)}, u32[]{:S(2)}) copy-start(s32[128]{0:T(128)} %param.9) | copy-start | bytes 1540
  145.5 8.9 %copy-start.3 = (bf16[128,4096]{1,0:T(8,128)(2,1)S(1)}, bf16[128,4096]{1,0:T(8,128)(2,1)}, u32[]{:S(2)}) copy-start(bf16[128,4096]{1,0:T(8,128)(2,1)} %param.10) | copy-start | bytes 3145732
  170.1 26.2 %copy-start.4 = (f32[96,128]{1,0:T(8,128)S(1)}, f32[96,128]{1,0:T(8,128)}, u32[]{:S(2)}) copy-start(f32[96,128]{1,0:T(8,128)} %convolution_bitcast_fusion.block) | copy-start | bytes 147460
  177.2 67.7 %copy-start.1 = (bf16[32,128,1,128]{3,1,0,2:T(8,128)(2,1)S(1)}, bf16[32,128,1,128]{3,1,0,2:T(8,128)(2,1)}, u32[]{:S(2)}) copy-start(bf16[32,128,1,128]{3,1,0,2:T(8,128)(2,1)} %copy.24) | copy-start | bytes 3145732
Sparse Core Ops, SparseCore 0:
  11.1 134.2 all-gather.2

commit v2 on v1

--- a/solution.py
+++ b/solution.py
@@ -11,11 +11,13 @@
 MESH = pl.DeviceIdType.MESH
 
 
-def greet(peers):
+def greet(peers, tok_peers=()):
     barrier = pltpu.get_barrier_semaphore()
     for peer in peers:
         pl.semaphore_signal(barrier, inc=1, device_id={"vocab": peer}, device_id_type=MESH)
-    pl.semaphore_wait(barrier, len(peers))
+    for peer in tok_peers:
+        pl.semaphore_signal(barrier, inc=1, device_id={"tok": peer}, device_id_type=MESH)
+    pl.semaphore_wait(barrier, len(peers) + len(tok_peers))
 
 
 def gather_kernel(chips, block, out, send, recv, pass_send, pass_recv, keep):
@@ -74,37 +76,154 @@
     )(block)
 
 
-def exchange_kernel(count, blocks, out, send, recv, keep):
+def exchange_kernel(
+    count, n_tok, blocks, pooled, out, columns, send, recv, tok_send, tok_recv, keep
+):
     me = lax.axis_index("vocab")
+    row = lax.axis_index("tok")
     ahead = [lax.rem(me + step, count) for step in range(1, count)]
-    greet(ahead)
-    own = pltpu.make_async_copy(blocks.at[me], out.at[me], keep)
-    own.start()
-    copies = []
+    rows_ahead = [lax.rem(row + step, n_tok) for step in range(1, n_tok)]
+    part = columns.shape[2]
+    each = pooled.shape[2] // part
+
+    def column_block(index):
+        start = pl.multiple_of(lax.rem(index, each) * part, part)
+        return pooled.at[lax.div(index, each), :, pl.ds(start, part)]
+
+    greet(ahead, rows_ahead)
+    copies = [
+        pltpu.make_async_copy(blocks.at[me], out.at[me], keep.at[0]),
+        pltpu.make_async_copy(column_block(row), columns.at[row], keep.at[1]),
+    ]
     for step in sorted(range(1, count), key=lambda step: -min(step, count - step)):
-        copy = pltpu.make_async_remote_copy(
-            src_ref=blocks.at[ahead[step - 1]], dst_ref=out.at[me],
-            send_sem=send.at[step], recv_sem=recv.at[step],
-            device_id={"vocab": ahead[step - 1]}, device_id_type=MESH,
-        )
+        copies.append(
+            pltpu.make_async_remote_copy(
+                src_ref=blocks.at[ahead[step - 1]], dst_ref=out.at[me],
+                send_sem=send.at[step], recv_sem=recv.at[step],
+                device_id={"vocab": ahead[step - 1]}, device_id_type=MESH,
+            )
+        )
+    for step in range(1, n_tok):
+        copies.append(
+            pltpu.make_async_remote_copy(
+                src_ref=column_block(rows_ahead[step - 1]), dst_ref=columns.at[row],
+                send_sem=tok_send.at[step], recv_sem=tok_recv.at[step],
+                device_id={"tok": rows_ahead[step - 1]}, device_id_type=MESH,
+            )
+        )
+    for copy in copies:
         copy.start()
-        copies.append(copy)
     for copy in copies:
         copy.wait()
+
+
+def exchange(blocks, pooled, collective_id):
+    count = lax.axis_size("vocab")
+    n_tok = lax.axis_size("tok")
+    rows = pooled.shape[1]
+    part = pooled.shape[0] * pooled.shape[2] // n_tok
+    return pl.pallas_call(
+        functools.partial(exchange_kernel, count, n_tok),
+        out_shape=(
+            jax.ShapeDtypeStruct(blocks.shape, blocks.dtype),
+            jax.ShapeDtypeStruct((n_tok, rows, part), pooled.dtype),
+        ),
+        in_specs=[pl.BlockSpec(memory_space=pltpu.VMEM)] * 2,
+        out_specs=[pl.BlockSpec(memory_space=pltpu.VMEM)] * 2,
+        scratch_shapes=[pltpu.SemaphoreType.DMA((count,))] * 2
+        + [pltpu.SemaphoreType.DMA((n_tok,))] * 2
+        + [pltpu.SemaphoreType.DMA((2,))],
+        compiler_params=pltpu.CompilerParams(collective_id=collective_id, has_side_effects=True),
+        cost_estimate=pl.CostEstimate(flops=0, bytes_accessed=30_000_000, transcendentals=0),
+    )(blocks, pooled)
+
+
+SIDE_X = 4
+
+
+def tok_gather_kernel(
+    n_z, split, block, out, x_send, x_recv, z_send, z_recv, xz_send, xz_recv, zx_send, zx_recv, keep
+):
+    me = lax.axis_index("tok")
+    n_x = SIDE_X
+    x = lax.rem(me, n_x)
+    z = lax.div(me, n_x)
+    x_ahead = [z * n_x + lax.rem(x + step, n_x) for step in range(n_x)]
+    x_behind = [z * n_x + lax.rem(x + n_x - step, n_x) for step in range(n_x)]
+    z_ahead = [lax.rem(z + step, n_z) * n_x + x for step in range(n_z)]
+    z_behind = [lax.rem(z + n_z - step, n_z) * n_x + x for step in range(n_z)]
+    greet([], x_ahead[1:] + z_ahead[1:])
+    first = pl.ds(0, split)
+    second = pl.ds(split, block.shape[0] - split)
+    far_first = sorted(range(1, n_z), key=lambda step: -min(step, n_z - step))
+
+    def copy(source, index, rows, send, recv, peer):
+        made = pltpu.make_async_remote_copy(
+            src_ref=source, dst_ref=out.at[index, rows], send_sem=send, recv_sem=recv,
+            device_id={"tok": peer}, device_id_type=MESH,
+        )
+        made.start()
+        return made
+
+    own = pltpu.make_async_copy(block, out.at[me], keep)
+    own.start()
+    along_x = {
+        e: copy(block.at[first], me, first, x_send.at[e], x_recv.at[e], x_ahead[e])
+        for e in range(1, n_x)
+    }
+    along_z = {
+        d: copy(block.at[second], me, second, z_send.at[d], z_recv.at[d], z_ahead[d])
+        for d in far_first
+    }
+    later = []
+
+    def onward_z(source, index, e):
+        for d in far_first:
+            slot = e * n_z + d
+            later.append(
+                copy(source, index, first, xz_send.at[slot], xz_recv.at[slot], z_ahead[d])
+            )
+
+    def onward_x(source, index, d):
+        for e in (2, 1, 3):
+            slot = d * n_x + e
+            later.append(
+                copy(source, index, second, zx_send.at[slot], zx_recv.at[slot], x_ahead[e])
+            )
+
+    onward_x(block.at[second], me, 0)
+    onward_z(block.at[first], me, 0)
+    arrivals = [("x", 1), ("x", 3), ("z", 1), ("z", 7), ("x", 2), ("z", 2), ("z", 6)]
+    arrivals += [("z", 3), ("z", 5), ("z", 4)]
+    for axis, step in arrivals:
+        if axis == "x":
+            along_x[step].wait_recv()
+            onward_z(out.at[x_behind[step], first], x_behind[step], step)
+        else:
+            along_z[step].wait_recv()
+            onward_x(out.at[z_behind[step], second], z_behind[step], step)
+    for made in later:
+        made.wait()
+    for made in list(along_x.values()) + list(along_z.values()):
+        made.wait_send()
     own.wait()
 
 
-def vocab_exchange(blocks, collective_id):
-    count = lax.axis_size("vocab")
+def tok_gather(block, collective_id):
+    n_tok = lax.axis_size("tok")
+    n_z = n_tok // SIDE_X
     return pl.pallas_call(
-        functools.partial(exchange_kernel, count),
-        out_shape=jax.ShapeDtypeStruct(blocks.shape, blocks.dtype),
+        functools.partial(tok_gather_kernel, n_z, block.shape[0] // 3),
+        out_shape=jax.ShapeDtypeStruct((n_tok,) + block.shape, block.dtype),
         in_specs=[pl.BlockSpec(memory_space=pltpu.VMEM)],
         out_specs=pl.BlockSpec(memory_space=pltpu.VMEM),
-        scratch_shapes=[pltpu.SemaphoreType.DMA((count,))] * 2 + [pltpu.SemaphoreType.DMA],
+        scratch_shapes=[pltpu.SemaphoreType.DMA((SIDE_X,))] * 2
+        + [pltpu.SemaphoreType.DMA((n_z,))] * 2
+        + [pltpu.SemaphoreType.DMA((n_tok,))] * 4
+        + [pltpu.SemaphoreType.DMA],
         compiler_params=pltpu.CompilerParams(collective_id=collective_id, has_side_effects=True),
         cost_estimate=pl.CostEstimate(flops=0, bytes_accessed=30_000_000, transcendentals=0),
-    )(blocks)
+    )(block)
 
 
 def padded(cells, axis, width):
@@ -142,8 +261,8 @@
     counts = (ends - starts).astype(jnp.float32)
     pooled_part = (summed / counts[:, None]).astype(jnp.bfloat16)
     part = pooled_part.shape[1]
-    pooled = vocab_gather(pooled_part, 0)
-    pooled = jnp.swapaxes(pooled, 0, 1).reshape(rows, n_vocab * part)
+    pooled_blocks = vocab_gather(pooled_part, 0)
+    pooled = jnp.swapaxes(pooled_blocks, 0, 1).reshape(rows, n_vocab * part)
     projected_part = lax.dot_general(
         proj_weight, pooled, (((1,), (1,)), ((), ())), preferred_element_type=jnp.float32
     )
@@ -152,10 +271,6 @@
     projected = vocab_gather(projected_part, 1).reshape(width, rows)
     inverse = lax.rsqrt(jnp.sum(projected * projected, axis=0) / width + EPS)
     normed = (projected * inverse[None, :] * norm_gain[:, None]).astype(jnp.bfloat16)
-    column_part = n_vocab * part // n_tok
-    pooled_columns = lax.all_to_all(
-        pooled.reshape(rows, n_tok, column_part), "tok", 1, 0, tiled=True
-    ).reshape(n_tok * rows, column_part)
 
     student = student_logits.astype(jnp.float32)
     head_logits = lax.dot_general(
@@ -201,7 +316,9 @@
     grad_parts = lax.dot_general(
         head_full, logit_grad, (((0,), (1,)), ((), ())), preferred_element_type=jnp.float32
     ).astype(jnp.bfloat16)
-    grad_parts = vocab_exchange(grad_parts.reshape(n_vocab, width_part, rows), 3)
+    grad_parts, pooled_columns = exchange(
+        grad_parts.reshape(n_vocab, width_part, rows), pooled_blocks, 3
+    )
     normed_grad = jnp.sum(grad_parts.astype(jnp.float32), axis=0)
     gain_part = lax.dynamic_slice_in_dim(
         norm_gain, lax.axis_index("vocab") * width_part, width_part
@@ -211,9 +328,13 @@
     out_grad = (inverse[None, :] * (gain_grad - scaled_part * inner[None, :] / width)).astype(
         jnp.bfloat16
     )
-    out_grads = lax.all_gather(out_grad, "tok", axis=0)
-    out_grads = jnp.swapaxes(out_grads, 0, 1).reshape(width_part, n_tok * rows)
-    proj_grad = jnp.dot(out_grads, pooled_columns, preferred_element_type=jnp.float32)
+    out_grads = tok_gather(out_grad, 4)
+    proj_grad = lax.dot_general(
+        jnp.swapaxes(out_grads, 0, 1).reshape(width_part, n_tok * rows),
+        pooled_columns.reshape(n_tok * rows, -1),
+        (((1,), (0,)), ((), ())),
+        preferred_element_type=jnp.float32,
+    )
     return (token_loss, proj_grad)
 
 

time: 254 us -> 240 us (0.945)
  the two profiles are of different devices: /device:TPU:8 before, /device:TPU:1 now
where the time goes in v2:
time: 240 us; the launch traced here: 238 us
  Pallas kernels  105 us (44%)
  waiting for transfers between devices  76.4 us (32%)
  matrix products  21.1 us (9%)
  between operations  14.2 us (6%)
  other arithmetic  11.1 us (5%)
  starting transfers between devices  5.25 us (2%)
  local copies, waits for them, and re-layouts  4.71 us (2%)
    all_gather x1, waiting for transfers between devices, on_device(): head_full = lax.all_gather(head_weight, 'tok', axis=0, tiled=True)  75.5 us
    pallas_call x3, Pallas kernels, vocab_gather(): pl.pallas_call(functools.partial(gather_kernel, chips), out_shape=jax.Sha...  53.5 us
    pallas_call x1, Pallas kernels, exchange(): pl.pallas_call(functools.partial(exchange_kernel, count, n_tok), out_shap...  31.8 us
    pallas_call x1, Pallas kernels, tok_gather(): pl.pallas_call(functools.partial(tok_gather_kernel, n_z, block.shape[0] /...  20 us
    dot_general x1, matrix products, on_device(): lax.dot_general(normed, head_full, (((0,), (1,)), ((), ())), preferred_el...  8.91 us
    dot_general x1, matrix products, on_device(): lax.dot_general(head_full, logit_grad, (((0,), (1,)), ((), ())), preferre...  7.04 us
  transfers between devices with their start and end apart: 3, of which 2 were waited for; matrix products, arithmetic and copies ran while one was open for 5% of the time, Pallas kernels for 17%

profile of v2, /device:TPU:1, one launch (start us, length us, event | category | flops | bytes accessed | tf_op | source)
XLA Modules:
  0.0 238.1 jit_solution(1099676441658317145)
XLA Ops:
  7.2 0.0 copy-start
  7.2 0.0 all-gather.2.cloned.1.call-start
  7.2 0.7 all-gather.2.cloned.1.call-update
  7.9 0.7 fusion.38
  8.7 3.9 %collective-permute-start = (bf16[32,256]{1,0:T(8,128)(2,1)S(1)}, bf16[32,256]{1,0:T(8,128)(2,1)S(1)}, u32[]{:S(2)}, u32[]{:S(2)}) collective-permute-start(bf16[32,256]{1,0:T(8,128)(2,1)S(1)} %get-tuple-element.29), channel_id=1, source_target_pairs={{0,16},{16,32},{32,48},{48,64},{64,80},{80,96},{96,112},{112,128},... | collective-permute-start | bytes 49160 | tf_op jit(solution)/shard_map/ppermute | solution.py:236
  12.6 1.3 collective-permute-start.1
  13.9 1.4 reduce_max.36
  15.4 0.8 slice_bitcast_fusion.3
  16.1 0.8 dynamic_slice.3
  16.9 0.0 collective-permute-done
  16.9 0.2 collective-permute-done.1
  17.1 1.7 fusion.13.block
  18.7 23.1 %shard_map.86.pooled = bf16[16,128,256]{2,1,0:T(8,128)(2,1)} custom-call(bf16[128,256]{1,0:T(8,128)(2,1)} %fusion.13.block), custom_call_target="tpu_custom_call" | custom-call | bytes 30000000 | tf_op jit(solution)/shard_map/pallas_call | solution.py:68
  41.8 1.6 copy.15
  43.4 0.0 copy-start.3
  43.4 0.0 copy-done
  43.5 1.0 convolution_bitcast_fusion.block
  44.4 18.1 %shard_map.87 = f32[16,96,128]{2,1,0:T(8,128)} custom-call(f32[96,128]{1,0:T(8,128)} %convolution_bitcast_fusion.block), custom_call_target="tpu_custom_call" | custom-call | bytes 30000000 | tf_op jit(solution)/shard_map/pallas_call | solution.py:68
  62.6 1.4 multiply_reduce_fusion.1
  64.0 0.0 copy-done.3
  64.0 1.4 fusion.22
  65.4 0.0 copy-start.4
  65.4 75.5 %all-gather.2.cloned.1.call-done = bf16[4096,1536]{1,0:T(8,128)(2,1)} async-done(((bf16[128,1536]{1,0:T(8,128)(2,1)}), bf16[4096,1536]{1,0:T(8,128)(2,1)}) %all-gather.2.cloned.1.call-update) | async-done | bytes 12582928 | tf_op jit(solution)/shard_map/all_gather | solution.py:249
  140.9 0.0 copy-start.1
  140.9 8.9 %fusion.40 = (f32[128]{0:T(128)S(1)}, f32[128,4096]{1,0:T(8,128)S(1)}) fusion(bf16[1536,128]{1,0:T(8,128)(2,1)S(1)} %fusion.22, bf16[4096,1536]{1,0:T(8,128)(2,1)} %all-gather.2.cloned.1.call-done), kind=kOutput, calls=%fused_computation.75 | convolution fusion | flops 1611136896 | bytes 15073792 | tf_op jit(solution)/shard_map/dot_general | solution.py:276
  149.8 0.0 copy-done.4
  149.8 0.0 copy-done.1
  149.8 1.7 multiply_reduce_fusion
  151.5 0.6 stack.32.block
  152.2 12.3 %shard_map.88 = f32[16,8,128]{2,1,0:T(8,128)} custom-call(f32[8,128]{1,0:T(8,128)} %stack.32.block), custom_call_target="tpu_custom_call" | custom-call | bytes 30000000 | tf_op jit(solution)/shard_map/pallas_call | solution.py:68
  164.5 1.3 fusion.37
  165.8 0.9 reduce_max.41
  166.7 0.5 fusion.34
  167.2 7.0 %fusion = bf16[1536,128]{0,1:T(8,128)(2,1)S(1)} fusion(bf16[4096,1536]{1,0:T(8,128)(2,1)} %all-gather.2.cloned.1.call-done, bf16[128,4096]{1,0:T(8,128)(2,1)} %param.10, f32[128,4096]{1,0:T(8,128)S(1)} %get-tuple-element.41, f32[128]{0:T(128)S(1)} %get-tuple-element.31, f32[128]{0:T(128)S(1)} %get-tuple-element.20, s32[4096]{0:T(1024)S(1)} %iota_add_fusion, ...), kind=kOutput, calls=%fused_computation.6 | convolution fusion | flops 1615527936 | bytes 16139776 | tf_op jit(solution)/shard_map/dot_general | solution.py:316
  174.3 0.0 copy-start.2
  174.3 0.9 copy.21
  175.2 31.8 %shard_map.89 = (bf16[16,96,128]{2,1,0:T(8,128)(2,1)}, bf16[32,128,128]{2,1,0:T(8,128)(2,1)}) custom-call(bf16[16,96,128]{2,1,0:T(8,128)(2,1)} %bitcast.69, bf16[16,128,256]{2,1,0:T(8,128)(2,1)} %shard_map.86.pooled), custom_call_target="tpu_custom_call" | custom-call | bytes 30000000 | tf_op jit(solution)/shard_map/pallas_call | solution.py:125
  207.0 1.1 convert_reduce_fusion
  208.1 0.0 copy-done.2
  208.1 0.7 multiply_convert_fusion.block
  208.8 20.0 %shard_map.90 = bf16[32,96,128]{2,1,0:T(8,128)(2,1)} custom-call(bf16[96,128]{1,0:T(8,128)(2,1)} %multiply_convert_fusion.block), custom_call_target="tpu_custom_call" | custom-call | bytes 30000000 | tf_op jit(solution)/shard_map/pallas_call | solution.py:215
  228.8 2.5 %convolution_bitcast_fusion.1 = f32[96,128]{1,0:T(8,128)} fusion(bf16[32,128,128]{2,1,0:T(8,128)(2,1)} %get-tuple-element.5, bf16[32,96,128]{2,1,0:T(8,128)(2,1)} %shard_map.90), kind=kOutput, calls=%fused_computation.24 | convolution fusion | flops 100663296 | bytes 1884160 | tf_op jit(solution)/shard_map/dot_general | solution.py:332
  (6 shorter events, 0.1 us)
Async XLA Ops:
  7.2 36.3 %copy-start = (bf16[96,4096]{1,0:T(8,128)(2,1)S(1)}, bf16[96,4096]{1,0:T(8,128)(2,1)}, u32[]{:S(2)}) copy-start(bf16[96,4096]{1,0:T(8,128)(2,1)} %param.11) | copy-start | bytes 2359300
  7.2 133.7 %all-gather.2.cloned.1.call-start = ((), (), s32[]{:S(2)}) async-start(), calls=%async_computation | async-start | bytes 12976128 | tf_op jit(solution)/shard_map/all_gather | solution.py:249
  8.7 8.2 %collective-permute-start = (bf16[32,256]{1,0:T(8,128)(2,1)S(1)}, bf16[32,256]{1,0:T(8,128)(2,1)S(1)}, u32[]{:S(2)}, u32[]{:S(2)}) collective-permute-start(bf16[32,256]{1,0:T(8,128)(2,1)S(1)} %get-tuple-element.29), channel_id=1, source_target_pairs={{0,16},{16,32},{32,48},{48,64},{64,80},{80,96},{96,112},{112,128},... | collective-permute-start | bytes 49160 | tf_op jit(solution)/shard_map/ppermute | solution.py:236
  12.6 4.5 %collective-permute-start.1 = (bf16[32,256]{1,0:T(8,128)(2,1)S(1)}, bf16[32,256]{1,0:T(8,128)(2,1)S(1)}, u32[]{:S(2)}, u32[]{:S(2)}) collective-permute-start(bf16[32,256]{1,0:T(8,128)(2,1)S(1)} %get-tuple-element.30), channel_id=1, source_target_pairs={{16,0},{32,16},{48,32},{64,48},{80,64},{96,80},{112,96},{128,112},... | collective-permute-start | bytes 49160 | tf_op jit(solution)/shard_map/ppermute | solution.py:238
  43.4 20.5 %copy-start.3 = (f32[1536]{0:T(1024)S(1)}, f32[1536]{0:T(1024)}, u32[]{:S(2)}) copy-start(f32[1536]{0:T(1024)} %param.12) | copy-start | bytes 18436
  65.4 84.5 %copy-start.4 = (s32[128]{0:T(128)S(1)}, s32[128]{0:T(128)}, u32[]{:S(2)}) copy-start(s32[128]{0:T(128)} %param.9) | copy-start | bytes 1540
  140.9 8.9 %copy-start.1 = (bf16[128,4096]{1,0:T(8,128)(2,1)S(1)}, bf16[128,4096]{1,0:T(8,128)(2,1)}, u32[]{:S(2)}) copy-start(bf16[128,4096]{1,0:T(8,128)(2,1)} %param.10) | copy-start | bytes 3145732
  174.3 33.8 %copy-start.2 = (f32[96,128]{1,0:T(8,128)S(1)}, f32[96,128]{1,0:T(8,128)}, u32[]{:S(2)}) copy-start(f32[96,128]{1,0:T(8,128)} %convolution_bitcast_fusion.block) | copy-start | bytes 147460
Sparse Core Ops, SparseCore 0:
  11.1 129.7 all-gather.1

commit v3 on v2

--- a/solution.py
+++ b/solution.py
@@ -226,19 +226,185 @@
     )(block)
 
 
-def padded(cells, axis, width):
-    count = lax.axis_size(axis)
-    ends = count - 1
-    head = cells[:width]
-    tail = cells[cells.shape[0] - width :]
-    return jnp.concatenate(
-        [
-            lax.ppermute(tail, axis, [(i, (i + 1) % count) for i in range(ends)]),
-            cells,
-            lax.ppermute(head, axis, [((i + 1) % count, i) for i in range(ends)]),
-        ],
-        axis=0,
-    )
+def cycle_place(cycle, tok, n_z):
+    x = lax.rem(tok, SIDE_X)
+    z = lax.div(tok, SIDE_X)
+    turn = lax.rem(x + z, SIDE_X)
+    if cycle == 0:
+        return SIDE_X * z + turn
+    return SIDE_X * lax.rem(3 * (z + n_z - turn), n_z) + turn
+
+
+def cycle_device(cycle, place, n_z):
+    lap = lax.div(place, SIDE_X)
+    turn = lax.rem(place, SIDE_X)
+    if cycle == 0:
+        return SIDE_X * lap + lax.rem(turn + 2 * n_z - lap, SIDE_X)
+    return SIDE_X * lax.rem(3 * lap + turn, n_z) + lax.rem(lap, SIDE_X)
+
+
+def front_kernel(
+    chips, n_tok, teacher, spans, proj_weight, head,
+    head_full, pooled, projected,
+    extended, ring_send, ring_recv, halo_send, halo_recv,
+    y_send, y_recv, core_send, core_recv, keep,
+):
+    n_z = n_tok // SIDE_X
+    laps = n_tok - 1
+    tok = lax.axis_index("tok")
+    me = lax.axis_index("vocab")
+    core = lax.rem(me, 2)
+    chip = lax.div(me, 2)
+    partner = chip * 2 + (1 - core)
+    ahead = [lax.rem(chip + step, chips) * 2 + core for step in range(1, chips)]
+    behind = [lax.rem(chip + chips - step, chips) * 2 + core for step in range(1, chips)]
+    tok_next = lax.rem(tok + 1, n_tok)
+    tok_last = lax.rem(tok + n_tok - 1, n_tok)
+    places = [cycle_place(cycle, tok, n_z) for cycle in range(2)]
+    targets = []
+    for cycle in range(2):
+        targets.append(cycle_device(cycle, lax.rem(places[cycle] + 1, n_tok), n_z))
+        targets.append(cycle_device(cycle, lax.rem(places[cycle] + n_tok - 1, n_tok), n_z))
+    greet(ahead + [partner], targets + [tok_next, tok_last])
+
+    columns = head.shape[1] // 4
+
+    def share(ring):
+        return pl.ds(ring * columns, columns)
+
+    def ring_copy(ring, step, source=None):
+        back = n_tok - step if ring % 2 == 0 else step
+        cycle = ring // 2
+        owner = cycle_device(cycle, lax.rem(places[cycle] + back, n_tok), n_z)
+        block = head_full.at[owner, :, share(ring)]
+        return pltpu.make_async_remote_copy(
+            src_ref=block if source is None else source, dst_ref=block,
+            send_sem=ring_send.at[ring * laps + step], recv_sem=ring_recv.at[ring * laps + step],
+            device_id={"tok": targets[ring]}, device_id_type=MESH,
+        )
+
+    def ring_steps(low, high):
+        @pl.loop(low, high)
+        def _(step):
+            for ring in range(4):
+                ring_copy(ring, step - 1).wait_recv()
+                ring_copy(ring, step).start()
+
+    for ring in range(4):
+        ring_copy(ring, 0, head.at[:, share(ring)]).start()
+    rows = teacher.shape[0]
+    margin = rows // 4
+    halos = [
+        pltpu.make_async_remote_copy(
+            src_ref=teacher.at[pl.ds(rows - margin, margin)], dst_ref=extended.at[pl.ds(0, margin)],
+            send_sem=halo_send.at[0], recv_sem=halo_recv.at[0],
+            device_id={"tok": tok_next}, device_id_type=MESH,
+        ),
+        pltpu.make_async_remote_copy(
+            src_ref=teacher.at[pl.ds(0, margin)], dst_ref=extended.at[pl.ds(rows + margin, margin)],
+            send_sem=halo_send.at[1], recv_sem=halo_recv.at[1],
+            device_id={"tok": tok_last}, device_id_type=MESH,
+        ),
+    ]
+    for halo in halos:
+        halo.start()
+    own = pltpu.make_async_copy(head, head_full.at[tok], keep)
+    own.start()
+    extended[pl.ds(margin, rows), :] = teacher[...]
+    starts = spans[:, 0:1]
+    ends = spans[:, 1:2]
+    positions = (
+        tok * rows - margin + lax.broadcasted_iota(jnp.int32, (rows, rows + 2 * margin), 1)
+    )
+    member = jnp.where((positions >= starts) & (positions < ends), 1.0, 0.0).astype(jnp.bfloat16)
+    counts = (ends - starts).astype(jnp.float32)
+    ring_steps(1, 2)
+    for halo in halos:
+        halo.wait()
+    summed = jnp.dot(member, extended[...], preferred_element_type=jnp.float32)
+    pooled[me] = (summed / counts).astype(jnp.bfloat16)
+
+    far_first = sorted(range(1, chips), key=lambda step: -min(step, chips - step))
+
+    def vocab_copy(which, out, index, slot, send, recv, peer):
+        return pltpu.make_async_remote_copy(
+            src_ref=out.at[index], dst_ref=out.at[index],
+            send_sem=send.at[which * chips + slot], recv_sem=recv.at[which * chips + slot],
+            device_id={"vocab": peer}, device_id_type=MESH,
+        )
+
+    def spread(which, out):
+        copies = [
+            vocab_copy(which, out, me, step, y_send, y_recv, ahead[step - 1]) for step in far_first
+        ]
+        for copy in copies:
+            copy.start()
+        own_pass = vocab_copy(which, out, me, 0, core_send, core_recv, partner)
+        own_pass.start()
+        return copies, [own_pass]
+
+    def pass_on(which, out, copies, passes):
+        for copy, step in reversed(list(zip(copies, far_first))):
+            copy.wait_recv()
+            onward = vocab_copy(which, out, behind[step - 1], step, core_send, core_recv, partner)
+            onward.start()
+            passes.append(onward)
+
+    copies, passes = spread(0, pooled)
+    ring_steps(2, 7)
+    pass_on(0, pooled, copies, passes)
+    ring_steps(7, 8)
+    for onward in passes:
+        onward.wait()
+    part = pooled.shape[2]
+    total = None
+    for j in range(2 * chips):
+        term = lax.dot_general(
+            proj_weight[:, j * part : (j + 1) * part], pooled[j], (((1,), (1,)), ((), ())),
+            preferred_element_type=jnp.float32,
+        )
+        total = term if total is None else total + term
+    projected[me] = total
+    more, more_passes = spread(1, projected)
+    ring_steps(8, 13)
+    pass_on(1, projected, more, more_passes)
+    ring_steps(13, 14)
+    for onward in more_passes:
+        onward.wait()
+    ring_steps(14, laps)
+    for ring in range(4):
+        ring_copy(ring, laps - 1).wait_recv()
+
+    @pl.loop(0, laps)
+    def _(step):
+        for ring in range(4):
+            ring_copy(ring, step).wait_send()
+
+    for copy in copies + more:
+        copy.wait_send()
+    own.wait()
+
+
+def front(teacher, spans, proj_weight, head, collective_id):
+    n_tok = lax.axis_size("tok")
+    n_vocab = lax.axis_size("vocab")
+    chips = n_vocab // 2
+    rows, part = teacher.shape
+    sems = [4 * (n_tok - 1)] * 2 + [2] * 2 + [2 * chips] * 4
+    return pl.pallas_call(
+        functools.partial(front_kernel, chips, n_tok),
+        out_shape=(
+            jax.ShapeDtypeStruct((n_tok,) + head.shape, head.dtype),
+            jax.ShapeDtypeStruct((n_vocab, rows, part), jnp.bfloat16),
+            jax.ShapeDtypeStruct((n_vocab, proj_weight.shape[0], rows), jnp.float32),
+        ),
+        in_specs=[pl.BlockSpec(memory_space=pltpu.VMEM)] * 4,
+        out_specs=[pl.BlockSpec(memory_space=pl.ANY)] + [pl.BlockSpec(memory_space=pltpu.VMEM)] * 2,
+        scratch_shapes=[pltpu.VMEM((rows + rows // 2, part), jnp.bfloat16)]
+        + [pltpu.SemaphoreType.DMA((size,)) for size in sems]
+        + [pltpu.SemaphoreType.DMA],
+        compiler_params=pltpu.CompilerParams(collective_id=collective_id, has_side_effects=True),
+    )(teacher, spans, proj_weight, head)
 
 
 def on_device(
@@ -246,29 +412,17 @@
 ):
     n_tok = lax.axis_size("tok")
     n_vocab = lax.axis_size("vocab")
-    head_full = lax.all_gather(head_weight, "tok", axis=0, tiled=True)
     rows = teacher_hidden.shape[0]
-    margin = rows // 4
-    extended = padded(teacher_hidden, "tok", margin)
-    first_row = lax.axis_index("tok") * rows - margin
-    positions = first_row + jnp.arange(rows + 2 * margin, dtype=jnp.int32)
-    starts = span_table[:, 0]
-    ends = span_table[:, 1]
-    member = (
-        (positions[None, :] >= starts[:, None]) & (positions[None, :] < ends[:, None])
-    ).astype(jnp.bfloat16)
-    summed = jnp.dot(member, extended, preferred_element_type=jnp.float32)
-    counts = (ends - starts).astype(jnp.float32)
-    pooled_part = (summed / counts[:, None]).astype(jnp.bfloat16)
-    part = pooled_part.shape[1]
-    pooled_blocks = vocab_gather(pooled_part, 0)
-    pooled = jnp.swapaxes(pooled_blocks, 0, 1).reshape(rows, n_vocab * part)
-    projected_part = lax.dot_general(
-        proj_weight, pooled, (((1,), (1,)), ((), ())), preferred_element_type=jnp.float32
-    )
     width_part = proj_weight.shape[0]
+    head_full, pooled_blocks, projected = front(
+        teacher_hidden, span_table, proj_weight, head_weight, 0
+    )
+    head_full = head_full.reshape(-1, head_weight.shape[1])
+    projected_part = lax.dynamic_index_in_dim(
+        projected, lax.axis_index("vocab"), 0, keepdims=False
+    )
     width = norm_gain.shape[0]
-    projected = vocab_gather(projected_part, 1).reshape(width, rows)
+    projected = projected.reshape(width, rows)
     inverse = lax.rsqrt(jnp.sum(projected * projected, axis=0) / width + EPS)
     normed = (projected * inverse[None, :] * norm_gain[:, None]).astype(jnp.bfloat16)
 

time: 240 us -> 258 us (1.075)
  Pallas kernels: 105 us -> 224 us
  waiting for transfers between devices: 76.4 us -> 0 us
  between operations: 14.2 us -> 0.73 us
  starting transfers between devices: 5.25 us -> 0 us
    pallas_call x0 -> x1, Pallas kernels: none -> 145 us  [front(): pl.pallas_call(functools.partial(front_kernel, chips, n_tok), out_shape=(...]
    all_gather x1 -> x0, waiting for transfers between devices: 75.5 us -> none  [on_device(): head_full = lax.all_gather(head_weight, 'tok', axis=0, tiled=True)]
    pallas_call x3 -> x1, Pallas kernels: 53.5 us -> 28.2 us  [vocab_gather(): pl.pallas_call(functools.partial(gather_kernel, chips), out_shape=jax.Sha...]
    ppermute x2 -> x0, starting transfers between devices: 5.21 us -> none  [the longest x1 3.92 us: padded(): lax.ppermute(tail, axis, [(i, (i + 1) % count) for i in range(ends)])]
    dot_general x2 -> x0, matrix products: 2.66 us -> none  [the longest x1 1.68 us: on_device(): summed = jnp.dot(member, extended, preferred_element_type=jnp.float32)]
  transfers between devices with their start and end apart: 3 -> 0, of which waited for: 2 -> 0; matrix products, arithmetic and copies ran while one was open for 5% -> 0% of each run, Pallas kernels for 17% -> 0%
where the time goes in v3:
time: 258 us; the launch traced here: 255 us
  Pallas kernels  224 us (87%)
  matrix products  19 us (7%)
  other arithmetic  9.94 us (4%)
    pallas_call x1, Pallas kernels, front(): pl.pallas_call(functools.partial(front_kernel, chips, n_tok), out_shape=(...  145 us
    pallas_call x1, Pallas kernels, exchange(): pl.pallas_call(functools.partial(exchange_kernel, count, n_tok), out_shap...  31.4 us
    pallas_call x1, Pallas kernels, vocab_gather(): pl.pallas_call(functools.partial(gather_kernel, chips), out_shape=jax.Sha...  28.2 us
    pallas_call x1, Pallas kernels, tok_gather(): pl.pallas_call(functools.partial(tok_gather_kernel, n_z, block.shape[0] /...  19.3 us
    dot_general x1, matrix products, on_device(): lax.dot_general(normed, head_full, (((0,), (1,)), ((), ())), preferred_el...  8.96 us
    dot_general x1, matrix products, on_device(): lax.dot_general(head_full, logit_grad, (((0,), (1,)), ((), ())), preferre...  7.57 us

profile of v3, /device:TPU:1, one launch (start us, length us, event | category | flops | bytes accessed | tf_op | source)
XLA Modules:
  0.0 255.4 jit_solution(14810897146062361230)
XLA Ops:
  0.6 0.0 copy-start.1
  0.6 1.4 copy.9.spans
  2.0 144.6 %shard_map.86 = (bf16[32,128,1536]{2,1,0:T(8,128)(2,1)}, bf16[16,128,256]{2,1,0:T(8,128)(2,1)}, f32[16,96,128]{2,1,0:T(8,128)}) custom-call(bf16[128,256]{1,0:T(8,128)(2,1)} %teacher.1, s32[128,2]{1,0:T(8,128)} %copy.9.spans, bf16[96,4096]{1,0:T(8,128)(2,1)} %proj_weight.1, bf16[128,1536]{1,0:T(8,128)(2,1)} %head.1), custom_call_target="tpu_custom_call" | custom-call | tf_op jit(solution)/shard_map/pallas_call | solution.py:394
  146.7 1.4 multiply_reduce_fusion.1
  148.0 0.0 copy-done.1
  148.1 0.1 mul.106
  148.1 1.4 multiply_convert_fusion
  149.5 0.0 copy-start
  149.5 0.0 copy-start.2
  149.6 9.0 %fusion.28 = (f32[128]{0:T(128)S(1)}, f32[128,4096]{1,0:T(8,128)S(1)}) fusion(bf16[1536,128]{1,0:T(8,128)(2,1)S(1)} %bitcast.63, bf16[4096,1536]{1,0:T(8,128)(2,1)} %bitcast.61), kind=kOutput, calls=%fused_computation.57 | convolution fusion | flops 1611136896 | bytes 15073792 | tf_op jit(solution)/shard_map/dot_general | solution.py:430
  158.5 0.0 copy-done
  158.5 0.2 reduce_max.36
  158.8 0.0 copy-done.2
  158.8 1.7 multiply_reduce_fusion
  160.5 0.6 stack.32.block
  161.1 28.2 %shard_map.87 = f32[16,8,128]{2,1,0:T(8,128)} custom-call(f32[8,128]{1,0:T(8,128)} %stack.32.block), custom_call_target="tpu_custom_call" | custom-call | bytes 30000000 | tf_op jit(solution)/shard_map/pallas_call | solution.py:68
  189.3 1.3 fusion.26
  190.6 0.9 reduce_max.41
  191.5 0.5 fusion.24
  192.0 7.6 %convolution_convert_fusion = bf16[1536,128]{1,0:T(8,128)(2,1)} fusion(bf16[4096,1536]{1,0:T(8,128)(2,1)} %bitcast.62, bf16[128,4096]{1,0:T(8,128)(2,1)S(1)} %copy-done, f32[128,4096]{1,0:T(8,128)S(1)} %get-tuple-element.42, f32[128]{0:T(128)S(1)} %get-tuple-element.35, f32[128]{0:T(128)S(1)} %get-tuple-element.26, s32[4096]{0:T(1024)S(1)} %iota_add_fusion, ...), kind=kOutput, calls=%fused_computation.5 | convolution fusion | flops 1615527936 | bytes 16139776 | tf_op jit(solution)/shard_map/dot_general | solution.py:470
  199.6 31.4 %shard_map.88 = (bf16[16,96,128]{2,1,0:T(8,128)(2,1)}, bf16[32,128,128]{2,1,0:T(8,128)(2,1)}) custom-call(bf16[16,96,128]{2,1,0:T(8,128)(2,1)} %bitcast.64, bf16[16,128,256]{2,1,0:T(8,128)(2,1)} %get-tuple-element.9.pooled), custom_call_target="tpu_custom_call" | custom-call | bytes 30000000 | tf_op jit(solution)/shard_map/pallas_call | solution.py:125
  231.0 1.1 convert_reduce_fusion
  232.1 0.1 dynamic_slice.7
  232.2 1.5 fusion.23.block
  233.7 19.3 %shard_map.89 = bf16[32,96,128]{2,1,0:T(8,128)(2,1)} custom-call(bf16[96,128]{1,0:T(8,128)(2,1)} %fusion.23.block), custom_call_target="tpu_custom_call" | custom-call | bytes 30000000 | tf_op jit(solution)/shard_map/pallas_call | solution.py:215
  253.0 2.5 convolution_bitcast_fusion
  (5 shorter events, 0.1 us)
Async XLA Ops:
  0.6 147.4 %copy-start.1 = (f32[1536]{0:T(1024)S(1)}, f32[1536]{0:T(1024)}, u32[]{:S(2)}) copy-start(f32[1536]{0:T(1024)} %param.12) | copy-start | bytes 18436
  149.5 9.0 %copy-start = (bf16[128,4096]{1,0:T(8,128)(2,1)S(1)}, bf16[128,4096]{1,0:T(8,128)(2,1)}, u32[]{:S(2)}) copy-start(bf16[128,4096]{1,0:T(8,128)(2,1)} %param.10) | copy-start | bytes 3145732
  149.5 9.2 %copy-start.2 = (s32[128]{0:T(128)S(1)}, s32[128]{0:T(128)}, u32[]{:S(2)}) copy-start(s32[128]{0:T(128)} %param.9) | copy-start | bytes 1540

commit v4 on v3

--- a/solution.py
+++ b/solution.py
@@ -76,66 +76,37 @@
     )(block)
 
 
-def exchange_kernel(
-    count, n_tok, blocks, pooled, out, columns, send, recv, tok_send, tok_recv, keep
-):
+def exchange_kernel(count, blocks, out, send, recv, keep):
     me = lax.axis_index("vocab")
-    row = lax.axis_index("tok")
     ahead = [lax.rem(me + step, count) for step in range(1, count)]
-    rows_ahead = [lax.rem(row + step, n_tok) for step in range(1, n_tok)]
-    part = columns.shape[2]
-    each = pooled.shape[2] // part
-
-    def column_block(index):
-        start = pl.multiple_of(lax.rem(index, each) * part, part)
-        return pooled.at[lax.div(index, each), :, pl.ds(start, part)]
-
-    greet(ahead, rows_ahead)
-    copies = [
-        pltpu.make_async_copy(blocks.at[me], out.at[me], keep.at[0]),
-        pltpu.make_async_copy(column_block(row), columns.at[row], keep.at[1]),
-    ]
+    greet(ahead)
+    own = pltpu.make_async_copy(blocks.at[me], out.at[me], keep)
+    own.start()
+    copies = []
     for step in sorted(range(1, count), key=lambda step: -min(step, count - step)):
-        copies.append(
-            pltpu.make_async_remote_copy(
-                src_ref=blocks.at[ahead[step - 1]], dst_ref=out.at[me],
-                send_sem=send.at[step], recv_sem=recv.at[step],
-                device_id={"vocab": ahead[step - 1]}, device_id_type=MESH,
-            )
-        )
-    for step in range(1, n_tok):
-        copies.append(
-            pltpu.make_async_remote_copy(
-                src_ref=column_block(rows_ahead[step - 1]), dst_ref=columns.at[row],
-                send_sem=tok_send.at[step], recv_sem=tok_recv.at[step],
-                device_id={"tok": rows_ahead[step - 1]}, device_id_type=MESH,
-            )
-        )
-    for copy in copies:
+        copy = pltpu.make_async_remote_copy(
+            src_ref=blocks.at[ahead[step - 1]], dst_ref=out.at[me],
+            send_sem=send.at[step], recv_sem=recv.at[step],
+            device_id={"vocab": ahead[step - 1]}, device_id_type=MESH,
+        )
         copy.start()
+        copies.append(copy)
     for copy in copies:
         copy.wait()
-
-
-def exchange(blocks, pooled, collective_id):
+    own.wait()
+
+
+def vocab_exchange(blocks, collective_id):
     count = lax.axis_size("vocab")
-    n_tok = lax.axis_size("tok")
-    rows = pooled.shape[1]
-    part = pooled.shape[0] * pooled.shape[2] // n_tok
     return pl.pallas_call(
-        functools.partial(exchange_kernel, count, n_tok),
-        out_shape=(
-            jax.ShapeDtypeStruct(blocks.shape, blocks.dtype),
-            jax.ShapeDtypeStruct((n_tok, rows, part), pooled.dtype),
-        ),
-        in_specs=[pl.BlockSpec(memory_space=pltpu.VMEM)] * 2,
-        out_specs=[pl.BlockSpec(memory_space=pltpu.VMEM)] * 2,
-        scratch_shapes=[pltpu.SemaphoreType.DMA((count,))] * 2
-        + [pltpu.SemaphoreType.DMA((n_tok,))] * 2
-        + [pltpu.SemaphoreType.DMA((2,))],
+        functools.partial(exchange_kernel, count),
+        out_shape=jax.ShapeDtypeStruct(blocks.shape, blocks.dtype),
+        in_specs=[pl.BlockSpec(memory_space=pltpu.VMEM)],
+        out_specs=pl.BlockSpec(memory_space=pltpu.VMEM),
+        scratch_shapes=[pltpu.SemaphoreType.DMA((count,))] * 2 + [pltpu.SemaphoreType.DMA],
         compiler_params=pltpu.CompilerParams(collective_id=collective_id, has_side_effects=True),
         cost_estimate=pl.CostEstimate(flops=0, bytes_accessed=30_000_000, transcendentals=0),
-    )(blocks, pooled)
+    )(blocks)
 
 
 SIDE_X = 4
@@ -226,104 +197,117 @@
     )(block)
 
 
-def cycle_place(cycle, tok, n_z):
-    x = lax.rem(tok, SIDE_X)
-    z = lax.div(tok, SIDE_X)
-    turn = lax.rem(x + z, SIDE_X)
-    if cycle == 0:
-        return SIDE_X * z + turn
-    return SIDE_X * lax.rem(3 * (z + n_z - turn), n_z) + turn
-
-
-def cycle_device(cycle, place, n_z):
-    lap = lax.div(place, SIDE_X)
-    turn = lax.rem(place, SIDE_X)
-    if cycle == 0:
-        return SIDE_X * lap + lax.rem(turn + 2 * n_z - lap, SIDE_X)
-    return SIDE_X * lax.rem(3 * lap + turn, n_z) + lax.rem(lap, SIDE_X)
+ROW_TILE = 16
+
+
+def gather_plan(rows, split, n_x, n_z):
+    sides = {"x": n_x, "z": n_z}
+    free, arriving, plan, whole = {}, [], [], set()
+
+    def send(now, kind, offset, way, hop):
+        low, high = gather_rows(rows, split, sides[kind[0]], kind, offset, way, hop)
+        link = (kind[0], way)
+        free[link] = max(now, free.get(link, 0.0)) + 0.066 * (high - low)
+        arriving.append((free[link] + 2.0, len(plan), (kind, offset, way, hop)))
+        plan.append((now, "send", (kind, offset, way, hop)))
+
+    for kind in ("xa", "zb", "za", "xb"):
+        for way in range(2):
+            send(0.0, kind, 0, way, 1)
+    while arriving:
+        first = min(arriving)
+        arriving.remove(first)
+        now, _, (kind, offset, way, hop) = first
+        plan.append((now, "wait", (kind, offset, way, hop)))
+        side = sides[kind[0]]
+        if hop < side // 2:
+            send(now, kind, offset, way, hop + 1)
+        if kind in ("xa", "zb"):
+            found = hop if way == 0 else side - hop
+            if hop < side // 2 or kind in whole:
+                onward = "za" if kind == "xa" else "xb"
+                for way_on in range(2):
+                    send(now, onward, found, way_on, 1)
+            else:
+                whole.add(kind)
+    return plan
+
+
+def gather_rows(rows, split, side, kind, offset, way, hop):
+    low, high = (0, split) if kind[1] == "a" else (split, rows)
+    if hop == side // 2:
+        cut = (high - low) // (2 * ROW_TILE) * ROW_TILE
+        middle = low + cut if offset % 2 == 0 else high - cut
+        return (low, middle) if way == 0 else (middle, high)
+    return low, high
 
 
 def front_kernel(
-    chips, n_tok, teacher, spans, proj_weight, head,
-    head_full, pooled, projected,
-    extended, ring_send, ring_recv, halo_send, halo_recv,
-    y_send, y_recv, core_send, core_recv, keep,
+    chips, n_tok, plan, teacher, spans, proj_weight, head,
+    head_full, pooled, projected, column_rows,
+    extended, head_send, head_recv, halo_send, halo_recv,
+    y_send, y_recv, core_send, core_recv,
+    tok_send, tok_recv, row_send, row_recv, keep,
 ):
-    n_z = n_tok // SIDE_X
-    laps = n_tok - 1
+    n_x = SIDE_X
+    n_z = n_tok // n_x
     tok = lax.axis_index("tok")
+    x = lax.rem(tok, n_x)
+    z = lax.div(tok, n_x)
     me = lax.axis_index("vocab")
     core = lax.rem(me, 2)
     chip = lax.div(me, 2)
     partner = chip * 2 + (1 - core)
     ahead = [lax.rem(chip + step, chips) * 2 + core for step in range(1, chips)]
     behind = [lax.rem(chip + chips - step, chips) * 2 + core for step in range(1, chips)]
-    tok_next = lax.rem(tok + 1, n_tok)
-    tok_last = lax.rem(tok + n_tok - 1, n_tok)
-    places = [cycle_place(cycle, tok, n_z) for cycle in range(2)]
-    targets = []
-    for cycle in range(2):
-        targets.append(cycle_device(cycle, lax.rem(places[cycle] + 1, n_tok), n_z))
-        targets.append(cycle_device(cycle, lax.rem(places[cycle] + n_tok - 1, n_tok), n_z))
-    greet(ahead + [partner], targets + [tok_next, tok_last])
-
-    columns = head.shape[1] // 4
-
-    def share(ring):
-        return pl.ds(ring * columns, columns)
-
-    def ring_copy(ring, step, source=None):
-        back = n_tok - step if ring % 2 == 0 else step
-        cycle = ring // 2
-        owner = cycle_device(cycle, lax.rem(places[cycle] + back, n_tok), n_z)
-        block = head_full.at[owner, :, share(ring)]
+    tok_ahead = [lax.rem(tok + step, n_tok) for step in range(1, n_tok)]
+    greet(ahead + [partner], tok_ahead)
+
+    def device(x_back, z_back):
+        return lax.rem(z + n_z - z_back, n_z) * n_x + lax.rem(x + n_x - x_back, n_x)
+
+    rows = teacher.shape[0]
+    split = rows * 3 // 8 // ROW_TILE * ROW_TILE
+    slots = {name: slot for slot, name in enumerate(n for _, act, n in plan if act == "send")}
+    started = []
+
+    def head_copy(name, sending):
+        kind, offset, way, hop = name
+        side = n_x if kind[0] == "x" else n_z
+        low, high = gather_rows(rows, split, side, kind, offset, way, hop)
+        span = pl.ds(low, high - low)
+        along = hop - 1 if sending else hop
+        along = along % side if way == 0 else (side - along) % side
+        to = side - 1 if way == 0 else 1
+        if kind[0] == "x":
+            block, peer = device(along, offset), device(to, 0)
+        else:
+            block, peer = device(offset, along), device(0, to)
+        target = head_full.at[block, span]
+        own_block = sending and hop == 1 and offset == 0
         return pltpu.make_async_remote_copy(
-            src_ref=block if source is None else source, dst_ref=block,
-            send_sem=ring_send.at[ring * laps + step], recv_sem=ring_recv.at[ring * laps + step],
-            device_id={"tok": targets[ring]}, device_id_type=MESH,
-        )
-
-    def ring_steps(low, high):
-        @pl.loop(low, high)
-        def _(step):
-            for ring in range(4):
-                ring_copy(ring, step - 1).wait_recv()
-                ring_copy(ring, step).start()
-
-    for ring in range(4):
-        ring_copy(ring, 0, head.at[:, share(ring)]).start()
-    rows = teacher.shape[0]
+            src_ref=head.at[span] if own_block else target, dst_ref=target,
+            send_sem=head_send.at[slots[name]], recv_sem=head_recv.at[slots[name]],
+            device_id={"tok": peer}, device_id_type=MESH,
+        )
+
     margin = rows // 4
     halos = [
         pltpu.make_async_remote_copy(
             src_ref=teacher.at[pl.ds(rows - margin, margin)], dst_ref=extended.at[pl.ds(0, margin)],
             send_sem=halo_send.at[0], recv_sem=halo_recv.at[0],
-            device_id={"tok": tok_next}, device_id_type=MESH,
+            device_id={"tok": tok_ahead[0]}, device_id_type=MESH,
         ),
         pltpu.make_async_remote_copy(
             src_ref=teacher.at[pl.ds(0, margin)], dst_ref=extended.at[pl.ds(rows + margin, margin)],
             send_sem=halo_send.at[1], recv_sem=halo_recv.at[1],
-            device_id={"tok": tok_last}, device_id_type=MESH,
+            device_id={"tok": tok_ahead[-1]}, device_id_type=MESH,
         ),
     ]
     for halo in halos:
         halo.start()
-    own = pltpu.make_async_copy(head, head_full.at[tok], keep)
-    own.start()
-    extended[pl.ds(margin, rows), :] = teacher[...]
-    starts = spans[:, 0:1]
-    ends = spans[:, 1:2]
-    positions = (
-        tok * rows - margin + lax.broadcasted_iota(jnp.int32, (rows, rows + 2 * margin), 1)
-    )
-    member = jnp.where((positions >= starts) & (positions < ends), 1.0, 0.0).astype(jnp.bfloat16)
-    counts = (ends - starts).astype(jnp.float32)
-    ring_steps(1, 2)
-    for halo in halos:
-        halo.wait()
-    summed = jnp.dot(member, extended[...], preferred_element_type=jnp.float32)
-    pooled[me] = (summed / counts).astype(jnp.bfloat16)
-
+    own_head = pltpu.make_async_copy(head, head_full.at[tok], keep.at[0])
+    own_head.start()
     far_first = sorted(range(1, chips), key=lambda step: -min(step, chips - step))
 
     def vocab_copy(which, out, index, slot, send, recv, peer):
@@ -350,39 +334,98 @@
             onward.start()
             passes.append(onward)
 
-    copies, passes = spread(0, pooled)
-    ring_steps(2, 7)
-    pass_on(0, pooled, copies, passes)
-    ring_steps(7, 8)
-    for onward in passes:
-        onward.wait()
     part = pooled.shape[2]
-    total = None
-    for j in range(2 * chips):
-        term = lax.dot_general(
-            proj_weight[:, j * part : (j + 1) * part], pooled[j], (((1,), (1,)), ((), ())),
-            preferred_element_type=jnp.float32,
-        )
-        total = term if total is None else total + term
-    projected[me] = total
-    more, more_passes = spread(1, projected)
-    ring_steps(8, 13)
-    pass_on(1, projected, more, more_passes)
-    ring_steps(13, 14)
-    for onward in more_passes:
-        onward.wait()
-    ring_steps(14, laps)
-    for ring in range(4):
-        ring_copy(ring, laps - 1).wait_recv()
-
-    @pl.loop(0, laps)
-    def _(step):
-        for ring in range(4):
-            ring_copy(ring, step).wait_send()
-
-    for copy in copies + more:
+    piece = column_rows.shape[3]
+    each = part // piece
+    few = column_rows.shape[2]
+    kept = {}
+
+    def pool():
+        extended[pl.ds(margin, rows), :] = teacher[...]
+        starts = spans[:, 0:1]
+        ends = spans[:, 1:2]
+        positions = (
+            tok * rows - margin + lax.broadcasted_iota(jnp.int32, (rows, rows + 2 * margin), 1)
+        )
+        inside = (positions >= starts) & (positions < ends)
+        member = jnp.where(inside, 1.0, 0.0).astype(jnp.bfloat16)
+        counts = (ends - starts).astype(jnp.float32)
+        for halo in halos:
+            halo.wait()
+        summed = jnp.dot(member, extended[...], preferred_element_type=jnp.float32)
+        pooled[me] = (summed / counts).astype(jnp.bfloat16)
+        kept["pooled"] = spread(0, pooled)
+
+    def pass_pooled():
+        pass_on(0, pooled, *kept["pooled"])
+
+    def pooled_piece(index):
+        start = pl.multiple_of(lax.rem(index, each) * piece, piece)
+        first = pl.multiple_of(chip * few, few)
+        return pooled.at[lax.div(index, each), pl.ds(first, few), pl.ds(start, piece)]
+
+    def project():
+        for onward in kept["pooled"][1]:
+            onward.wait()
+        total = None
+        for j in range(2 * chips):
+            term = lax.dot_general(
+                proj_weight[:, j * part : (j + 1) * part], pooled[j], (((1,), (1,)), ((), ())),
+                preferred_element_type=jnp.float32,
+            )
+            total = term if total is None else total + term
+        projected[me] = total
+        kept["projected"] = spread(1, projected)
+        pieces = []
+        for step in range(1, n_tok):
+            pieces.append(
+                pltpu.make_async_remote_copy(
+                    src_ref=pooled_piece(tok_ahead[step - 1]), dst_ref=column_rows.at[chip, tok],
+                    send_sem=tok_send.at[step], recv_sem=tok_recv.at[step],
+                    device_id={"tok": tok_ahead[step - 1]}, device_id_type=MESH,
+                )
+            )
+        pieces.append(
+            pltpu.make_async_copy(pooled_piece(tok), column_rows.at[chip, tok], keep.at[1])
+        )
+        for copy in pieces:
+            copy.start()
+        kept["pieces"] = pieces
+
+    def pass_projected():
+        pass_on(1, projected, *kept["projected"])
+
+    def gather_columns():
+        for onward in kept["projected"][1]:
+            onward.wait()
+        for copy in kept["pieces"]:
+            copy.wait()
+        kept["columns"] = []
+        for step in far_first:
+            copy = vocab_copy(0, column_rows, chip, step, row_send, row_recv, ahead[step - 1])
+            copy.start()
+            kept["columns"].append(copy)
+
+    jobs = [
+        (4.0, pool), (15.0, pass_pooled), (20.0, project), (33.0, pass_projected),
+        (40.0, gather_columns),
+    ]
+    for now, act, name in plan:
+        while jobs and jobs[0][0] <= now:
+            jobs.pop(0)[1]()
+        copy = head_copy(name, act == "send")
+        if act == "send":
+            copy.start()
+            started.append(copy)
+        else:
+            copy.wait_recv()
+    while jobs:
+        jobs.pop(0)[1]()
+    for copy in kept["columns"]:
+        copy.wait()
+    for copy in started + kept["pooled"][0] + kept["projected"][0]:
         copy.wait_send()
-    own.wait()
+    own_head.wait()
 
 
 def front(teacher, spans, proj_weight, head, collective_id):
@@ -390,19 +433,24 @@
     n_vocab = lax.axis_size("vocab")
     chips = n_vocab // 2
     rows, part = teacher.shape
-    sems = [4 * (n_tok - 1)] * 2 + [2] * 2 + [2 * chips] * 4
+    split = rows * 3 // 8 // ROW_TILE * ROW_TILE
+    plan = gather_plan(rows, split, SIDE_X, n_tok // SIDE_X)
+    moves = len(plan) // 2
+    sems = [moves] * 2 + [2] * 2 + [2 * chips] * 4 + [n_tok] * 2 + [chips] * 2 + [2]
     return pl.pallas_call(
-        functools.partial(front_kernel, chips, n_tok),
+        functools.partial(front_kernel, chips, n_tok, plan),
         out_shape=(
             jax.ShapeDtypeStruct((n_tok,) + head.shape, head.dtype),
             jax.ShapeDtypeStruct((n_vocab, rows, part), jnp.bfloat16),
             jax.ShapeDtypeStruct((n_vocab, proj_weight.shape[0], rows), jnp.float32),
+            jax.ShapeDtypeStruct(
+                (chips, n_tok, rows // chips, part * n_vocab // n_tok), jnp.bfloat16
+            ),
         ),
         in_specs=[pl.BlockSpec(memory_space=pltpu.VMEM)] * 4,
-        out_specs=[pl.BlockSpec(memory_space=pl.ANY)] + [pl.BlockSpec(memory_space=pltpu.VMEM)] * 2,
+        out_specs=[pl.BlockSpec(memory_space=pl.ANY)] + [pl.BlockSpec(memory_space=pltpu.VMEM)] * 3,
         scratch_shapes=[pltpu.VMEM((rows + rows // 2, part), jnp.bfloat16)]
-        + [pltpu.SemaphoreType.DMA((size,)) for size in sems]
-        + [pltpu.SemaphoreType.DMA],
+        + [pltpu.SemaphoreType.DMA((size,)) for size in sems],
         compiler_params=pltpu.CompilerParams(collective_id=collective_id, has_side_effects=True),
     )(teacher, spans, proj_weight, head)
 
@@ -414,7 +462,7 @@
     n_vocab = lax.axis_size("vocab")
     rows = teacher_hidden.shape[0]
     width_part = proj_weight.shape[0]
-    head_full, pooled_blocks, projected = front(
+    head_full, _, projected, column_rows = front(
         teacher_hidden, span_table, proj_weight, head_weight, 0
     )
     head_full = head_full.reshape(-1, head_weight.shape[1])
@@ -470,9 +518,7 @@
     grad_parts = lax.dot_general(
         head_full, logit_grad, (((0,), (1,)), ((), ())), preferred_element_type=jnp.float32
     ).astype(jnp.bfloat16)
-    grad_parts, pooled_columns = exchange(
-        grad_parts.reshape(n_vocab, width_part, rows), pooled_blocks, 3
-    )
+    grad_parts = vocab_exchange(grad_parts.reshape(n_vocab, width_part, rows), 3)
     normed_grad = jnp.sum(grad_parts.astype(jnp.float32), axis=0)
     gain_part = lax.dynamic_slice_in_dim(
         norm_gain, lax.axis_index("vocab") * width_part, width_part
@@ -485,7 +531,7 @@
     out_grads = tok_gather(out_grad, 4)
     proj_grad = lax.dot_general(
         jnp.swapaxes(out_grads, 0, 1).reshape(width_part, n_tok * rows),
-        pooled_columns.reshape(n_tok * rows, -1),
+        jnp.swapaxes(column_rows, 0, 1).reshape(n_tok * rows, -1),
         (((1,), (0,)), ((), ())),
         preferred_element_type=jnp.float32,
     )

time: 258 us -> 173 us (0.67)
  Pallas kernels: 224 us -> 140 us
    pallas_call x2, Pallas kernels: 176 us -> 108 us  [the longest x1 90.9 us: front(): pl.pallas_call(functools.partial(front_kernel, chips, n_tok, plan), out_s...]
    pallas_call x1, Pallas kernels: 28.2 us -> 13.4 us  [vocab_gather(): pl.pallas_call(functools.partial(gather_kernel, chips), out_shape=jax.Sha...]
where the time goes in v4:
time: 173 us; the launch traced here: 171 us
  Pallas kernels  140 us (81%)
  matrix products  17.6 us (10%)
  other arithmetic  9.93 us (6%)
  local copies, waits for them, and re-layouts  3.31 us (2%)
    pallas_call x1, Pallas kernels, front(): pl.pallas_call(functools.partial(front_kernel, chips, n_tok, plan), out_s...  90.9 us
    pallas_call x1, Pallas kernels, tok_gather(): pl.pallas_call(functools.partial(tok_gather_kernel, n_z, block.shape[0] /...  18.2 us
    pallas_call x1, Pallas kernels, vocab_exchange(): pl.pallas_call(functools.partial(exchange_kernel, count), out_shape=jax.S...  17.4 us
    pallas_call x1, Pallas kernels, vocab_gather(): pl.pallas_call(functools.partial(gather_kernel, chips), out_shape=jax.Sha...  13.4 us
    dot_general x1, matrix products, on_device(): lax.dot_general(normed, head_full, (((0,), (1,)), ((), ())), preferred_el...  8.96 us
    dot_general x1, matrix products, on_device(): lax.dot_general(head_full, logit_grad, (((0,), (1,)), ((), ())), preferre...  7.58 us

profile of v4, /device:TPU:1, one launch (start us, length us, event | category | flops | bytes accessed | tf_op | source)
XLA Modules:
  0.0 171.5 jit_solution(13204736026815769571)
XLA Ops:
  0.6 0.0 copy-start.3
  0.6 1.4 copy.15.spans
  2.0 90.9 %shard_map.86 = (bf16[32,128,1536]{2,1,0:T(8,128)(2,1)}, bf16[16,128,256]{2,1,0:T(8,128)(2,1)}, f32[16,96,128]{2,1,0:T(8,128)}, bf16[8,32,16,128]{3,2,1,0:T(8,128)(2,1)}) custom-call(bf16[128,256]{1,0:T(8,128)(2,1)} %teacher.1, s32[128,2]{1,0:T(8,128)} %copy.15.spans, bf16[96,4096]{1,0:T(8,128)(2,1)} %proj_weight.1, bf16[128,1536]{1,0:T(8,128)(2,1)} %head.1), custom_call_target="tpu_custom_call" | custom-call | tf_op jit(solution)/shard_map/pallas_call | solution.py:440
  92.9 1.4 multiply_reduce_fusion.1
  94.3 0.0 copy-done.3
  94.3 0.1 mul.106
  94.4 1.4 multiply_convert_fusion
  95.8 0.0 copy-start
  95.8 0.0 copy-start.4
  95.8 9.0 %fusion.30 = (f32[128]{0:T(128)S(1)}, f32[128,4096]{1,0:T(8,128)S(1)}) fusion(bf16[1536,128]{1,0:T(8,128)(2,1)S(1)} %bitcast.69, bf16[4096,1536]{1,0:T(8,128)(2,1)} %bitcast.66), kind=kOutput, calls=%fused_computation.58 | convolution fusion | flops 1611136896 | bytes 15073792 | tf_op jit(solution)/shard_map/dot_general | solution.py:478
  104.8 0.0 copy-done
  104.8 0.2 reduce_max.36
  105.0 0.0 copy-done.4
  105.0 1.7 multiply_reduce_fusion
  106.7 0.6 stack.32.block
  107.3 13.4 %shard_map.87 = f32[16,8,128]{2,1,0:T(8,128)} custom-call(f32[8,128]{1,0:T(8,128)} %stack.32.block), custom_call_target="tpu_custom_call" | custom-call | bytes 30000000 | tf_op jit(solution)/shard_map/pallas_call | solution.py:68
  120.7 1.3 fusion.28
  122.0 0.9 reduce_max.41
  122.9 0.5 fusion.26
  123.4 7.6 %convolution_convert_fusion = bf16[1536,128]{1,0:T(8,128)(2,1)} fusion(bf16[4096,1536]{1,0:T(8,128)(2,1)} %bitcast.67, bf16[128,4096]{1,0:T(8,128)(2,1)S(1)} %copy-done, f32[128,4096]{1,0:T(8,128)S(1)} %get-tuple-element.38, f32[128]{0:T(128)S(1)} %get-tuple-element.31, f32[128]{0:T(128)S(1)} %get-tuple-element.22, s32[4096]{0:T(1024)S(1)} %iota_add_fusion, ...), kind=kOutput, calls=%fused_computation.5 | convolution fusion | flops 1615527936 | bytes 16139776 | tf_op jit(solution)/shard_map/dot_general | solution.py:518
  131.0 0.0 copy-start.2
  131.0 17.4 %shard_map.88 = bf16[16,96,128]{2,1,0:T(8,128)(2,1)} custom-call(bf16[16,96,128]{2,1,0:T(8,128)(2,1)} %bitcast.71), custom_call_target="tpu_custom_call" | custom-call | bytes 30000000 | tf_op jit(solution)/shard_map/pallas_call | solution.py:101
  148.5 1.1 convert_reduce_fusion
  149.5 0.1 dynamic_slice.7
  149.6 1.5 fusion.25.block
  151.1 18.2 %shard_map.89 = bf16[32,96,128]{2,1,0:T(8,128)(2,1)} custom-call(bf16[96,128]{1,0:T(8,128)(2,1)} %fusion.25.block), custom_call_target="tpu_custom_call" | custom-call | bytes 30000000 | tf_op jit(solution)/shard_map/pallas_call | solution.py:186
  169.3 0.0 copy-start.1
  169.3 0.0 copy-done.2
  169.4 0.3 copy.22
  169.7 0.8 copy-done.1
  170.5 1.0 fusion.18
  (5 shorter events, 0.1 us)
Async XLA Ops:
  0.6 93.7 %copy-start.3 = (f32[1536]{0:T(1024)S(1)}, f32[1536]{0:T(1024)}, u32[]{:S(2)}) copy-start(f32[1536]{0:T(1024)} %param.12) | copy-start | bytes 18436
  95.8 9.0 %copy-start = (bf16[128,4096]{1,0:T(8,128)(2,1)S(1)}, bf16[128,4096]{1,0:T(8,128)(2,1)}, u32[]{:S(2)}) copy-start(bf16[128,4096]{1,0:T(8,128)(2,1)} %param.10) | copy-start | bytes 3145732
  95.8 9.2 %copy-start.4 = (s32[128]{0:T(128)S(1)}, s32[128]{0:T(128)}, u32[]{:S(2)}) copy-start(s32[128]{0:T(128)} %param.9) | copy-start | bytes 1540
  131.0 38.3 %copy-start.2 = (bf16[8,32,16,128]{3,2,1,0:T(8,128)(2,1)S(1)}, bf16[8,32,16,128]{3,2,1,0:T(8,128)(2,1)}, u32[]{:S(2)}) copy-start(bf16[8,32,16,128]{3,2,1,0:T(8,128)(2,1)} %get-tuple-element.7) | copy-start | bytes 3145732
  169.3 1.1 copy-start.1

commit v5 on v4

--- a/solution.py
+++ b/solution.py
@@ -20,181 +20,175 @@
     pl.semaphore_wait(barrier, len(peers) + len(tok_peers))
 
 
-def gather_kernel(chips, block, out, send, recv, pass_send, pass_recv, keep):
-    me = lax.axis_index("vocab")
-    core = lax.rem(me, 2)
-    chip = lax.div(me, 2)
-    partner = chip * 2 + (1 - core)
-    ahead = [lax.rem(chip + step, chips) * 2 + core for step in range(1, chips)]
-    behind = [lax.rem(chip + chips - step, chips) * 2 + core for step in range(1, chips)]
-    greet(ahead + [partner])
-    steps = sorted(range(1, chips), key=lambda step: -min(step, chips - step))
-    copies = {}
-    for step in steps:
-        copies[step] = pltpu.make_async_remote_copy(
-            src_ref=block, dst_ref=out.at[me], send_sem=send.at[step], recv_sem=recv.at[step],
-            device_id={"vocab": ahead[step - 1]}, device_id_type=MESH,
-        )
-        copies[step].start()
-    own = pltpu.make_async_copy(block, out.at[me], keep)
-    own.start()
-    passes = [
-        pltpu.make_async_remote_copy(
-            src_ref=block, dst_ref=out.at[me], send_sem=pass_send.at[0], recv_sem=pass_recv.at[0],
-            device_id={"vocab": partner}, device_id_type=MESH,
-        )
-    ]
-    passes[0].start()
-    for step in reversed(steps):
-        copies[step].wait_recv()
-        source = behind[step - 1]
-        onward = pltpu.make_async_remote_copy(
-            src_ref=out.at[source], dst_ref=out.at[source],
-            send_sem=pass_send.at[step], recv_sem=pass_recv.at[step],
-            device_id={"vocab": partner}, device_id_type=MESH,
-        )
-        onward.start()
-        passes.append(onward)
-    for onward in passes:
-        onward.wait()
-    for step in steps:
-        copies[step].wait_send()
-    own.wait()
-
-
-def vocab_gather(block, collective_id):
-    count = lax.axis_size("vocab")
-    chips = count // 2
-    return pl.pallas_call(
-        functools.partial(gather_kernel, chips),
-        out_shape=jax.ShapeDtypeStruct((count,) + block.shape, block.dtype),
-        in_specs=[pl.BlockSpec(memory_space=pltpu.VMEM)],
-        out_specs=pl.BlockSpec(memory_space=pltpu.VMEM),
-        scratch_shapes=[pltpu.SemaphoreType.DMA((chips,))] * 4 + [pltpu.SemaphoreType.DMA],
-        compiler_params=pltpu.CompilerParams(collective_id=collective_id, has_side_effects=True),
-        cost_estimate=pl.CostEstimate(flops=0, bytes_accessed=30_000_000, transcendentals=0),
-    )(block)
-
-
-def exchange_kernel(count, blocks, out, send, recv, keep):
+def merge_kernel(count, stats, out, held, send, recv, keep):
     me = lax.axis_index("vocab")
     ahead = [lax.rem(me + step, count) for step in range(1, count)]
     greet(ahead)
-    own = pltpu.make_async_copy(blocks.at[me], out.at[me], keep)
-    own.start()
-    copies = []
+    copies = [pltpu.make_async_copy(stats, held.at[me], keep)]
     for step in sorted(range(1, count), key=lambda step: -min(step, count - step)):
-        copy = pltpu.make_async_remote_copy(
-            src_ref=blocks.at[ahead[step - 1]], dst_ref=out.at[me],
-            send_sem=send.at[step], recv_sem=recv.at[step],
-            device_id={"vocab": ahead[step - 1]}, device_id_type=MESH,
+        copies.append(
+            pltpu.make_async_remote_copy(
+                src_ref=stats, dst_ref=held.at[me], send_sem=send.at[step], recv_sem=recv.at[step],
+                device_id={"vocab": ahead[step - 1]}, device_id_type=MESH,
+            )
         )
+    for copy in copies:
         copy.start()
-        copies.append(copy)
     for copy in copies:
         copy.wait()
-    own.wait()
-
-
-def vocab_exchange(blocks, collective_id):
+
+    def row(index):
+        return held[:, index, :]
+
+    def total(values):
+        return jnp.sum(values, axis=0, keepdims=True)
+
+    student_top = jnp.max(row(0), axis=0, keepdims=True)
+    head_top = jnp.max(row(4), axis=0, keepdims=True)
+    student_scale = jnp.exp(row(0) - student_top)
+    head_scale = jnp.exp(row(4) - head_top)
+    student_total = total(row(1) * student_scale)
+    student_gap = total(row(2) * student_scale) / student_total
+    student_head = total(row(3) * student_scale) / student_total
+    head_total = total(row(5) * head_scale)
+    head_head = total(row(6) * head_scale) / head_total
+    picked = total(row(7))
+    student_lse = student_top + jnp.log(student_total)
+    head_lse = head_top + jnp.log(head_total)
+    out[0:1, :] = student_lse
+    out[1:2, :] = head_lse
+    out[2:3, :] = student_gap - student_lse + head_lse + head_lse - picked
+    out[3:4, :] = 2.0 * head_head - student_head - picked
+    out[4:8, :] = jnp.zeros_like(out[4:8, :])
+
+
+def vocab_merge(stats, collective_id):
     count = lax.axis_size("vocab")
     return pl.pallas_call(
-        functools.partial(exchange_kernel, count),
-        out_shape=jax.ShapeDtypeStruct(blocks.shape, blocks.dtype),
+        functools.partial(merge_kernel, count),
+        out_shape=jax.ShapeDtypeStruct(stats.shape, stats.dtype),
         in_specs=[pl.BlockSpec(memory_space=pltpu.VMEM)],
         out_specs=pl.BlockSpec(memory_space=pltpu.VMEM),
-        scratch_shapes=[pltpu.SemaphoreType.DMA((count,))] * 2 + [pltpu.SemaphoreType.DMA],
+        scratch_shapes=[pltpu.VMEM((count,) + stats.shape, stats.dtype)]
+        + [pltpu.SemaphoreType.DMA((count,))] * 2
+        + [pltpu.SemaphoreType.DMA],
         compiler_params=pltpu.CompilerParams(collective_id=collective_id, has_side_effects=True),
-        cost_estimate=pl.CostEstimate(flops=0, bytes_accessed=30_000_000, transcendentals=0),
-    )(blocks)
+    )(stats)
 
 
 SIDE_X = 4
 
 
-def tok_gather_kernel(
-    n_z, split, block, out, x_send, x_recv, z_send, z_recv, xz_send, xz_recv, zx_send, zx_recv, keep
+def tail_kernel(
+    count, n_z, blocks, gain, inverse, shift, out,
+    parts, send, recv, x_send, x_recv, z_send, z_recv, on_send, on_recv, keep,
 ):
-    me = lax.axis_index("tok")
+    me = lax.axis_index("vocab")
+    ahead = [lax.rem(me + step, count) for step in range(1, count)]
+    tok = lax.axis_index("tok")
     n_x = SIDE_X
-    x = lax.rem(me, n_x)
-    z = lax.div(me, n_x)
+    n_tok = n_x * n_z
+    x = lax.rem(tok, n_x)
+    z = lax.div(tok, n_x)
     x_ahead = [z * n_x + lax.rem(x + step, n_x) for step in range(n_x)]
     x_behind = [z * n_x + lax.rem(x + n_x - step, n_x) for step in range(n_x)]
     z_ahead = [lax.rem(z + step, n_z) * n_x + x for step in range(n_z)]
     z_behind = [lax.rem(z + n_z - step, n_z) * n_x + x for step in range(n_z)]
-    greet([], x_ahead[1:] + z_ahead[1:])
-    first = pl.ds(0, split)
-    second = pl.ds(split, block.shape[0] - split)
-    far_first = sorted(range(1, n_z), key=lambda step: -min(step, n_z - step))
-
-    def copy(source, index, rows, send, recv, peer):
+    greet(ahead, x_ahead[1:] + z_ahead[1:])
+    each = blocks.shape[1] // 3
+    pieces = [pl.ds(piece * each, each) for piece in range(3)]
+    z_order = sorted(range(1, n_z), key=lambda step: -min(step, n_z - step))
+    x_order = sorted(range(1, n_x), key=lambda step: -min(step, n_x - step))
+    own = pltpu.make_async_copy(blocks.at[me], parts.at[me], keep)
+    own.start()
+    exchanged = []
+    for piece in range(3):
+        copies = []
+        for step in sorted(range(1, count), key=lambda step: -min(step, count - step)):
+            copies.append(
+                pltpu.make_async_remote_copy(
+                    src_ref=blocks.at[ahead[step - 1], pieces[piece]],
+                    dst_ref=parts.at[me, pieces[piece]],
+                    send_sem=send.at[piece * count + step], recv_sem=recv.at[piece * count + step],
+                    device_id={"vocab": ahead[step - 1]}, device_id_type=MESH,
+                )
+            )
+            copies[-1].start()
+        exchanged.append(copies)
+    own.wait()
+    first_hops = [{}, {}, {}]
+    later = []
+
+    def copy(index, piece, sends, recvs, slot, peer):
+        block = out.at[index, pieces[piece]]
         made = pltpu.make_async_remote_copy(
-            src_ref=source, dst_ref=out.at[index, rows], send_sem=send, recv_sem=recv,
+            src_ref=block, dst_ref=block, send_sem=sends.at[slot], recv_sem=recvs.at[slot],
             device_id={"tok": peer}, device_id_type=MESH,
         )
         made.start()
         return made
 
-    own = pltpu.make_async_copy(block, out.at[me], keep)
-    own.start()
-    along_x = {
-        e: copy(block.at[first], me, first, x_send.at[e], x_recv.at[e], x_ahead[e])
-        for e in range(1, n_x)
-    }
-    along_z = {
-        d: copy(block.at[second], me, second, z_send.at[d], z_recv.at[d], z_ahead[d])
-        for d in far_first
-    }
-    later = []
-
-    def onward_z(source, index, e):
-        for d in far_first:
-            slot = e * n_z + d
-            later.append(
-                copy(source, index, first, xz_send.at[slot], xz_recv.at[slot], z_ahead[d])
-            )
-
-    def onward_x(source, index, d):
-        for e in (2, 1, 3):
-            slot = d * n_x + e
-            later.append(
-                copy(source, index, second, zx_send.at[slot], zx_recv.at[slot], x_ahead[e])
-            )
-
-    onward_x(block.at[second], me, 0)
-    onward_z(block.at[first], me, 0)
-    arrivals = [("x", 1), ("x", 3), ("z", 1), ("z", 7), ("x", 2), ("z", 2), ("z", 6)]
-    arrivals += [("z", 3), ("z", 5), ("z", 4)]
-    for axis, step in arrivals:
-        if axis == "x":
-            along_x[step].wait_recv()
-            onward_z(out.at[x_behind[step], first], x_behind[step], step)
+    def onward(index, piece, far):
+        base = piece * n_tok
+        if piece == 0:
+            for d in z_order:
+                later.append(copy(index, piece, on_send, on_recv, base + far * n_z + d, z_ahead[d]))
         else:
-            along_z[step].wait_recv()
-            onward_x(out.at[z_behind[step], second], z_behind[step], step)
+            for e in x_order:
+                later.append(copy(index, piece, on_send, on_recv, base + far * n_x + e, x_ahead[e]))
+
+    def reduce_piece(piece):
+        for made in exchanged[piece]:
+            made.wait_recv()
+        rows = slice(piece * each, (piece + 1) * each)
+        total = parts[0, rows, :].astype(jnp.float32)
+        for index in range(1, count):
+            total = total + parts[index, rows, :].astype(jnp.float32)
+        grad = inverse[...] * (total * gain[rows, :] - shift[rows, :])
+        out[tok, rows, :] = grad.astype(out.dtype)
+        if piece == 0:
+            for e in x_order:
+                first_hops[piece][e] = copy(tok, piece, x_send, x_recv, e, x_ahead[e])
+        else:
+            for d in z_order:
+                slot = piece * n_z + d
+                first_hops[piece][d] = copy(tok, piece, z_send, z_recv, slot, z_ahead[d])
+        onward(tok, piece, 0)
+
+    def pass_on(piece):
+        behind = x_behind if piece == 0 else z_behind
+        for step in reversed(x_order if piece == 0 else z_order):
+            first_hops[piece][step].wait_recv()
+            onward(behind[step], piece, step)
+
+    reduce_piece(0)
+    reduce_piece(1)
+    pass_on(0)
+    reduce_piece(2)
+    pass_on(1)
+    pass_on(2)
     for made in later:
         made.wait()
-    for made in list(along_x.values()) + list(along_z.values()):
-        made.wait_send()
-    own.wait()
-
-
-def tok_gather(block, collective_id):
+    for piece in range(3):
+        for made in list(first_hops[piece].values()) + exchanged[piece]:
+            made.wait_send()
+
+
+def tail(blocks, gain, inverse, shift, collective_id):
+    count = lax.axis_size("vocab")
     n_tok = lax.axis_size("tok")
     n_z = n_tok // SIDE_X
+    sems = [3 * count] * 2 + [SIDE_X] * 2 + [3 * n_z] * 2 + [3 * n_tok] * 2
     return pl.pallas_call(
-        functools.partial(tok_gather_kernel, n_z, block.shape[0] // 3),
-        out_shape=jax.ShapeDtypeStruct((n_tok,) + block.shape, block.dtype),
-        in_specs=[pl.BlockSpec(memory_space=pltpu.VMEM)],
+        functools.partial(tail_kernel, count, n_z),
+        out_shape=jax.ShapeDtypeStruct((n_tok,) + blocks.shape[1:], blocks.dtype),
+        in_specs=[pl.BlockSpec(memory_space=pltpu.VMEM)] * 4,
         out_specs=pl.BlockSpec(memory_space=pltpu.VMEM),
-        scratch_shapes=[pltpu.SemaphoreType.DMA((SIDE_X,))] * 2
-        + [pltpu.SemaphoreType.DMA((n_z,))] * 2
-        + [pltpu.SemaphoreType.DMA((n_tok,))] * 4
+        scratch_shapes=[pltpu.VMEM(blocks.shape, blocks.dtype)]
+        + [pltpu.SemaphoreType.DMA((size,)) for size in sems]
         + [pltpu.SemaphoreType.DMA],
         compiler_params=pltpu.CompilerParams(collective_id=collective_id, has_side_effects=True),
-        cost_estimate=pl.CostEstimate(flops=0, bytes_accessed=30_000_000, transcendentals=0),
-    )(block)
+    )(blocks, gain, inverse, shift)
 
 
 ROW_TILE = 16
@@ -497,20 +491,8 @@
             jnp.sum(hit * head_logits, axis=1),
         ]
     )
-    stats = vocab_gather(stats, 2)
-    tops = jnp.max(stats, axis=0)
-    student_scale = jnp.exp(stats[:, 0] - tops[0])
-    head_scale = jnp.exp(stats[:, 4] - tops[4])
-    student_total = jnp.sum(stats[:, 1] * student_scale, axis=0)
-    student_gap = jnp.sum(stats[:, 2] * student_scale, axis=0) / student_total
-    student_head = jnp.sum(stats[:, 3] * student_scale, axis=0) / student_total
-    head_total = jnp.sum(stats[:, 5] * head_scale, axis=0)
-    head_head = jnp.sum(stats[:, 6] * head_scale, axis=0) / head_total
-    picked = jnp.sum(stats[:, 7], axis=0)
-    student_lse = tops[0] + jnp.log(student_total)
-    head_lse = tops[4] + jnp.log(head_total)
-    token_loss = student_gap - student_lse + head_lse + head_lse - picked
-    inner = 2.0 * head_head - student_head - picked
+    merged = vocab_merge(stats, 1)
+    student_lse, head_lse, token_loss, inner = (merged[index] for index in range(4))
 
     prob_student = jnp.exp(student - student_lse[:, None])
     prob_head = jnp.exp(head_logits - head_lse[:, None])
@@ -518,17 +500,17 @@
     grad_parts = lax.dot_general(
         head_full, logit_grad, (((0,), (1,)), ((), ())), preferred_element_type=jnp.float32
     ).astype(jnp.bfloat16)
-    grad_parts = vocab_exchange(grad_parts.reshape(n_vocab, width_part, rows), 3)
-    normed_grad = jnp.sum(grad_parts.astype(jnp.float32), axis=0)
     gain_part = lax.dynamic_slice_in_dim(
         norm_gain, lax.axis_index("vocab") * width_part, width_part
     )
-    gain_grad = normed_grad * gain_part[:, None]
     scaled_part = projected_part * inverse[None, :]
-    out_grad = (inverse[None, :] * (gain_grad - scaled_part * inner[None, :] / width)).astype(
-        jnp.bfloat16
-    )
-    out_grads = tok_gather(out_grad, 4)
+    out_grads = tail(
+        grad_parts.reshape(n_vocab, width_part, rows),
+        gain_part[:, None],
+        inverse[None, :],
+        scaled_part * inner[None, :] / width,
+        2,
+    )
     proj_grad = lax.dot_general(
         jnp.swapaxes(out_grads, 0, 1).reshape(width_part, n_tok * rows),
         jnp.swapaxes(column_rows, 0, 1).reshape(n_tok * rows, -1),

time: 173 us -> 167 us (0.965)
  Pallas kernels: 140 us -> 136 us
  other arithmetic: 9.93 us -> 6.62 us
  local copies, waits for them, and re-layouts: 3.31 us -> 5.84 us
    pallas_call x3 -> x2, Pallas kernels: 49 us -> 45.3 us  [the longest x1 32.7 us: tail(): pl.pallas_call(functools.partial(tail_kernel, count, n_z), out_shape=jax....]
where the time goes in v5:
time: 167 us
  Pallas kernels  136 us (81%)
  matrix products  17.6 us (11%)
  other arithmetic  6.62 us (4%)
  local copies, waits for them, and re-layouts  5.84 us (3%)
    pallas_call x1, Pallas kernels, front(): pl.pallas_call(functools.partial(front_kernel, chips, n_tok, plan), out_s...  90.9 us
    pallas_call x1, Pallas kernels, tail(): pl.pallas_call(functools.partial(tail_kernel, count, n_z), out_shape=jax....  32.7 us
    pallas_call x1, Pallas kernels, vocab_merge(): pl.pallas_call(functools.partial(merge_kernel, count), out_shape=jax.Shap...  12.6 us
    dot_general x1, matrix products, on_device(): lax.dot_general(normed, head_full, (((0,), (1,)), ((), ())), preferred_el...  8.96 us
    dot_general x1, matrix products, on_device(): lax.dot_general(head_full, logit_grad, (((0,), (1,)), ((), ())), preferre...  7.59 us

profile of v5, /device:TPU:1, one launch (start us, length us, event | category | flops | bytes accessed | tf_op | source)
XLA Modules:
  0.0 166.9 jit_solution(8315249400355943812)
XLA Ops:
  0.6 0.0 copy-start.2
  0.6 1.4 copy.11.spans
  2.0 90.9 %shard_map.86 = (bf16[32,128,1536]{2,1,0:T(8,128)(2,1)}, bf16[16,128,256]{2,1,0:T(8,128)(2,1)}, f32[16,96,128]{2,1,0:T(8,128)}, bf16[8,32,16,128]{3,2,1,0:T(8,128)(2,1)}) custom-call(bf16[128,256]{1,0:T(8,128)(2,1)} %teacher.1, s32[128,2]{1,0:T(8,128)} %copy.11.spans, bf16[96,4096]{1,0:T(8,128)(2,1)} %proj_weight.1, bf16[128,1536]{1,0:T(8,128)(2,1)} %head.1), custom_call_target="tpu_custom_call" | custom-call | tf_op jit(solution)/shard_map/pallas_call | solution.py:434
  92.9 1.4 multiply_reduce_fusion.1
  94.3 0.5 fusion.24
  94.8 0.0 copy-done.2
  94.8 0.1 mul.69
  94.9 1.4 multiply_convert_fusion
  96.3 0.0 copy-start
  96.3 0.0 copy-start.3
  96.3 9.0 %fusion.26 = (f32[128]{0:T(128)S(1)}, f32[128,4096]{1,0:T(8,128)S(1)}) fusion(bf16[1536,128]{1,0:T(8,128)(2,1)S(1)} %bitcast.47, bf16[4096,1536]{1,0:T(8,128)(2,1)} %bitcast.44), kind=kOutput, calls=%fused_computation.44 | convolution fusion | flops 1611136896 | bytes 15073792 | tf_op jit(solution)/shard_map/dot_general | solution.py:472
  105.3 0.0 copy-done
  105.3 0.2 reduce_max.27
  105.6 0.0 copy-done.3
  105.6 1.7 %multiply_reduce_fusion = (f32[128]{0:T(128)S(1)}, f32[128]{0:T(128)S(1)}, f32[128]{0:T(128)S(1)}, f32[128]{0:T(128)S(1)}, f32[128]{0:T(128)S(1)}, /*index=5*/f32[128]{0:T(128)S(1)}) fusion(f32[128,4096]{1,0:T(8,128)S(1)} %get-tuple-element.25, f32[128]{0:T(128)S(1)} %get-tuple-element.24, s32[128]{0:T(128)S(1)} %copy-done.3, s32[4096]{0:T(1024)S(1)} %iota_add_fusion, ...), kind=kLoop, calls=%fused_computation.17 | loop fusion | flops 7863552 | bytes 3166720 | tf_op jit(solution)/shard_map/reduce_sum | solution.py:490
  107.2 0.6 stack.32.stats
  107.9 12.6 %shard_map.87 = f32[8,128]{1,0:T(8,128)} custom-call(f32[8,128]{1,0:T(8,128)} %stack.32.stats), custom_call_target="tpu_custom_call" | custom-call | tf_op jit(solution)/shard_map/pallas_call | solution.py:67
  120.5 1.3 slice_bitcast_fusion
  121.8 1.4 fusion.22.shift
  123.2 7.6 %convolution_convert_fusion = bf16[1536,128]{1,0:T(8,128)(2,1)} fusion(bf16[4096,1536]{1,0:T(8,128)(2,1)} %bitcast.45, bf16[128,4096]{1,0:T(8,128)(2,1)S(1)} %copy-done, f32[128,4096]{1,0:T(8,128)S(1)} %get-tuple-element.25, f32[128]{0:T(128)S(1)} %get-tuple-element.17, f32[128]{0:T(128)S(1)} %get-tuple-element.18, s32[4096]{0:T(1024)S(1)} %iota_add_fusion, ...), kind=kOutput, calls=%fused_computation.5 | convolution fusion | flops 1615527936 | bytes 16139776 | tf_op jit(solution)/shard_map/dot_general | solution.py:500
  130.8 0.1 dynamic-slice_bitcast_fusion
  130.9 0.7 copy.12.gain
  131.6 32.7 %shard_map.88 = bf16[32,96,128]{2,1,0:T(8,128)(2,1)} custom-call(bf16[16,96,128]{2,1,0:T(8,128)(2,1)} %bitcast.49, f32[96,1]{1,0:T(8,128)} %copy.12.gain, f32[1,128]{1,0:T(1,128)} %get-tuple-element.20.inverse, f32[96,128]{1,0:T(8,128)} %fusion.22.shift), custom_call_target="tpu_custom_call" | custom-call | tf_op jit(solution)/shard_map/pallas_call | solution.py:182
  164.3 0.0 copy-start.1
  164.3 1.6 copy.14
  165.9 0.0 copy-done.1
  165.9 1.0 fusion.18
  (2 shorter events, 0.0 us)
Async XLA Ops:
  0.6 94.2 %copy-start.2 = (f32[1536]{0:T(1024)S(1)}, f32[1536]{0:T(1024)}, u32[]{:S(2)}) copy-start(f32[1536]{0:T(1024)} %param.12) | copy-start | bytes 18436
  96.3 9.0 %copy-start = (bf16[128,4096]{1,0:T(8,128)(2,1)S(1)}, bf16[128,4096]{1,0:T(8,128)(2,1)}, u32[]{:S(2)}) copy-start(bf16[128,4096]{1,0:T(8,128)(2,1)} %param.10) | copy-start | bytes 3145732
  96.3 9.2 %copy-start.3 = (s32[128]{0:T(128)S(1)}, s32[128]{0:T(128)}, u32[]{:S(2)}) copy-start(s32[128]{0:T(128)} %param.9) | copy-start | bytes 1540
  164.3 1.6 copy-start.1

commit v6 on v5

--- a/solution.py
+++ b/solution.py
@@ -336,18 +336,22 @@
 
     def pool():
         extended[pl.ds(margin, rows), :] = teacher[...]
-        starts = spans[:, 0:1]
-        ends = spans[:, 1:2]
+        starts = spans[0:1, :]
+        ends = spans[1:2, :]
         positions = (
-            tok * rows - margin + lax.broadcasted_iota(jnp.int32, (rows, rows + 2 * margin), 1)
+            tok * rows - margin + lax.broadcasted_iota(jnp.int32, (rows + 2 * margin, rows), 0)
         )
         inside = (positions >= starts) & (positions < ends)
         member = jnp.where(inside, 1.0, 0.0).astype(jnp.bfloat16)
-        counts = (ends - starts).astype(jnp.float32)
+        ones = jnp.ones((rows + 2 * margin, rows), jnp.bfloat16)
+        over_rows = (((0,), (0,)), ((), ()))
+        counts = lax.dot_general(member, ones, over_rows, preferred_element_type=jnp.float32)
         for halo in halos:
             halo.wait()
-        summed = jnp.dot(member, extended[...], preferred_element_type=jnp.float32)
-        pooled[me] = (summed / counts).astype(jnp.bfloat16)
+        summed = lax.dot_general(
+            member, extended[...], over_rows, preferred_element_type=jnp.float32
+        )
+        pooled[me] = (summed / counts[:, 0:1]).astype(jnp.bfloat16)
         kept["pooled"] = spread(0, pooled)
 
     def pass_pooled():
@@ -374,13 +378,13 @@
         for step in range(1, n_tok):
             pieces.append(
                 pltpu.make_async_remote_copy(
-                    src_ref=pooled_piece(tok_ahead[step - 1]), dst_ref=column_rows.at[chip, tok],
+                    src_ref=pooled_piece(tok_ahead[step - 1]), dst_ref=column_rows.at[tok, chip],
                     send_sem=tok_send.at[step], recv_sem=tok_recv.at[step],
                     device_id={"tok": tok_ahead[step - 1]}, device_id_type=MESH,
                 )
             )
         pieces.append(
-            pltpu.make_async_copy(pooled_piece(tok), column_rows.at[chip, tok], keep.at[1])
+            pltpu.make_async_copy(pooled_piece(tok), column_rows.at[tok, chip], keep.at[1])
         )
         for copy in pieces:
             copy.start()
@@ -396,7 +400,11 @@
             copy.wait()
         kept["columns"] = []
         for step in far_first:
-            copy = vocab_copy(0, column_rows, chip, step, row_send, row_recv, ahead[step - 1])
+            copy = pltpu.make_async_remote_copy(
+                src_ref=column_rows.at[:, chip], dst_ref=column_rows.at[:, chip],
+                send_sem=row_send.at[step], recv_sem=row_recv.at[step],
+                device_id={"vocab": ahead[step - 1]}, device_id_type=MESH,
+            )
             copy.start()
             kept["columns"].append(copy)
 
@@ -438,7 +446,7 @@
             jax.ShapeDtypeStruct((n_vocab, rows, part), jnp.bfloat16),
             jax.ShapeDtypeStruct((n_vocab, proj_weight.shape[0], rows), jnp.float32),
             jax.ShapeDtypeStruct(
-                (chips, n_tok, rows // chips, part * n_vocab // n_tok), jnp.bfloat16
+                (n_tok, chips, rows // chips, part * n_vocab // n_tok), jnp.bfloat16
             ),
         ),
         in_specs=[pl.BlockSpec(memory_space=pltpu.VMEM)] * 4,
@@ -457,7 +465,7 @@
     rows = teacher_hidden.shape[0]
     width_part = proj_weight.shape[0]
     head_full, _, projected, column_rows = front(
-        teacher_hidden, span_table, proj_weight, head_weight, 0
+        teacher_hidden, span_table.T, proj_weight, head_weight, 0
     )
     head_full = head_full.reshape(-1, head_weight.shape[1])
     projected_part = lax.dynamic_index_in_dim(
@@ -513,7 +521,7 @@
     )
     proj_grad = lax.dot_general(
         jnp.swapaxes(out_grads, 0, 1).reshape(width_part, n_tok * rows),
-        jnp.swapaxes(column_rows, 0, 1).reshape(n_tok * rows, -1),
+        column_rows.reshape(n_tok * rows, -1),
         (((1,), (0,)), ((), ())),
         preferred_element_type=jnp.float32,
     )

time: 167 us -> 167 us (level)
  no operation moved by 1% of the time
where the time goes in v6:
time: 167 us
  Pallas kernels  136 us (81%)
  matrix products  19 us (11%)
  other arithmetic  6.62 us (4%)
  local copies, waits for them, and re-layouts  4.23 us (3%)
    pallas_call x1, Pallas kernels, front(): pl.pallas_call(functools.partial(front_kernel, chips, n_tok, plan), out_s...  90.9 us
    pallas_call x1, Pallas kernels, tail(): pl.pallas_call(functools.partial(tail_kernel, count, n_z), out_shape=jax....  32.7 us
    pallas_call x1, Pallas kernels, vocab_merge(): pl.pallas_call(functools.partial(merge_kernel, count), out_shape=jax.Shap...  12.7 us
    dot_general x1, matrix products, on_device(): lax.dot_general(normed, head_full, (((0,), (1,)), ((), ())), preferred_el...  8.96 us
    dot_general x1, matrix products, on_device(): lax.dot_general(head_full, logit_grad, (((0,), (1,)), ((), ())), preferre...  7.58 us

profile of v6, /device:TPU:1, one launch (start us, length us, event | category | flops | bytes accessed | tf_op | source)
XLA Modules:
  0.0 166.8 jit_solution(10470548876202699689)
XLA Ops:
  0.6 90.9 %shard_map.86 = (bf16[32,128,1536]{2,1,0:T(8,128)(2,1)}, bf16[16,128,256]{2,1,0:T(8,128)(2,1)}, f32[16,96,128]{2,1,0:T(8,128)}, bf16[32,8,16,128]{3,2,1,0:T(8,128)(2,1)}) custom-call(bf16[128,256]{1,0:T(8,128)(2,1)} %teacher.1, s32[2,128]{1,0:T(2,128)} %bitcast.56, bf16[96,4096]{1,0:T(8,128)(2,1)} %proj_weight.1, bf16[128,1536]{1,0:T(8,128)(2,1)} %head.1), custom_call_target="tpu_custom_call" | custom-call | tf_op jit(solution)/shard_map/pallas_call | solution.py:442
  91.5 1.4 multiply_reduce_fusion.1
  92.9 0.5 fusion.24
  93.4 0.8 mul.69
  94.2 1.4 multiply_convert_fusion
  95.6 0.0 copy-start
  95.6 0.0 copy-start.1
  95.6 9.0 %fusion.26 = (f32[128]{0:T(128)S(1)}, f32[128,4096]{1,0:T(8,128)S(1)}) fusion(bf16[1536,128]{1,0:T(8,128)(2,1)S(1)} %bitcast.46, bf16[4096,1536]{1,0:T(8,128)(2,1)} %bitcast.44), kind=kOutput, calls=%fused_computation.44 | convolution fusion | flops 1611136896 | bytes 15073792 | tf_op jit(solution)/shard_map/dot_general | solution.py:480
  104.6 0.0 copy-done
  104.6 0.2 reduce_max.27
  104.8 0.0 copy-done.1
  104.8 1.7 %multiply_reduce_fusion = (f32[128]{0:T(128)S(1)}, f32[128]{0:T(128)S(1)}, f32[128]{0:T(128)S(1)}, f32[128]{0:T(128)S(1)}, f32[128]{0:T(128)S(1)}, /*index=5*/f32[128]{0:T(128)S(1)}) fusion(f32[128,4096]{1,0:T(8,128)S(1)} %get-tuple-element.25, f32[128]{0:T(128)S(1)} %get-tuple-element.24, s32[128]{0:T(128)S(1)} %copy-done.1, s32[4096]{0:T(1024)S(1)} %iota_add_fusion, ...), kind=kLoop, calls=%fused_computation.17 | loop fusion | flops 7863552 | bytes 3166720 | tf_op jit(solution)/shard_map/reduce_sum | solution.py:498
  106.5 0.6 stack.32.stats
  107.1 12.7 %shard_map.87 = f32[8,128]{1,0:T(8,128)} custom-call(f32[8,128]{1,0:T(8,128)} %stack.32.stats), custom_call_target="tpu_custom_call" | custom-call | tf_op jit(solution)/shard_map/pallas_call | solution.py:67
  119.8 1.3 slice_bitcast_fusion
  121.1 1.4 fusion.22.shift
  122.5 7.6 %convolution_convert_fusion = bf16[1536,128]{1,0:T(8,128)(2,1)} fusion(bf16[4096,1536]{1,0:T(8,128)(2,1)} %bitcast.45, bf16[128,4096]{1,0:T(8,128)(2,1)S(1)} %copy-done, f32[128,4096]{1,0:T(8,128)S(1)} %get-tuple-element.25, f32[128]{0:T(128)S(1)} %get-tuple-element.17, f32[128]{0:T(128)S(1)} %get-tuple-element.18, s32[4096]{0:T(1024)S(1)} %iota_add_fusion, ...), kind=kOutput, calls=%fused_computation.5 | convolution fusion | flops 1615527936 | bytes 16139776 | tf_op jit(solution)/shard_map/dot_general | solution.py:508
  130.1 0.8 dynamic-slice_bitcast_fusion
  130.9 0.7 copy.10.gain
  131.6 32.7 %shard_map.88 = bf16[32,96,128]{2,1,0:T(8,128)(2,1)} custom-call(bf16[16,96,128]{2,1,0:T(8,128)(2,1)} %bitcast.48, f32[96,1]{1,0:T(8,128)} %copy.10.gain, f32[1,128]{1,0:T(1,128)} %get-tuple-element.20.inverse, f32[96,128]{1,0:T(8,128)} %fusion.22.shift), custom_call_target="tpu_custom_call" | custom-call | tf_op jit(solution)/shard_map/pallas_call | solution.py:182
  164.4 2.5 %fusion.18 = f32[96,128]{1,0:T(8,128)} fusion(bf16[4096,128]{1,0:T(8,128)(2,1)} %bitcast.47, bf16[32,96,128]{2,1,0:T(8,128)(2,1)} %shard_map.88), kind=kOutput, calls=%fused_computation.25 | convolution fusion | flops 100663296 | bytes 1884160 | tf_op jit(solution)/shard_map/dot_general | solution.py:522
  (2 shorter events, 0.0 us)
Async XLA Ops:
  95.6 9.0 %copy-start = (bf16[128,4096]{1,0:T(8,128)(2,1)S(1)}, bf16[128,4096]{1,0:T(8,128)(2,1)}, u32[]{:S(2)}) copy-start(bf16[128,4096]{1,0:T(8,128)(2,1)} %param.10) | copy-start | bytes 3145732
  95.6 9.2 %copy-start.1 = (s32[128]{0:T(128)S(1)}, s32[128]{0:T(128)}, u32[]{:S(2)}) copy-start(s32[128]{0:T(128)} %param.9) | copy-start | bytes 1540
